TPU v7x, 128 devices: a whole 4x4x4 slice. The times are simulated.
128 devices in a mesh: pipe: 2 (over y_lo), tensor: 8 (over y_hi, x), dp: 8 (over z, core).
Axes of the slice: x: 4, y: 4 (y_hi: 2, y_lo: 2; y = y_hi * 2 + y_lo), z: 4, core: 2. Of those that a mesh axis runs over, the one named last changes fastest.
Arguments:
- section_input: bfloat16 [8192, 1024], P('dp'), may hold values from -6 to 6
- segment_ids: int32 [8192], P('dp'), may hold values from 0 to 127, never falling along the last dimension, each value on 1 to 256 neighbouring positions
- w_qkv: bfloat16 [2, 1024, 3, 1024], P('pipe', None, None, 'tensor'), may hold values from -0.1875 to 0.1875
- qv_bias: float32 [2, 2, 1024], P('pipe', None, 'tensor'), may hold values from -3 to 3
- w_out: bfloat16 [2, 1024, 1024], P('pipe', 'tensor'), may hold values from -0.75 to 0.75
- out_bias: float32 [2, 1024], P('pipe'), may hold values from -3 to 3
- w_up: bfloat16 [2, 1024, 4096], P('pipe', None, 'tensor'), may hold values from -0.1875 to 0.1875
- up_bias: float32 [2, 4096], P('pipe', 'tensor'), may hold values from -3 to 3
- w_down: bfloat16 [2, 4096, 1024], P('pipe', 'tensor'), may hold values from -0.09375 to 0.09375
- down_bias: float32 [2, 1024], P('pipe'), may hold values from -4 to 4
- norm_gains: float32 [2, 2, 1024], P('pipe'), may hold values from 0.25 to 1.75
- norm_shifts: float32 [2, 2, 1024], P('pipe'), may hold values from -2 to 2
- out_grad: bfloat16 [8192, 1024], P('dp'), may hold values from -6 to 6
Outputs:
- section_outputs: bfloat16 [2, 8192, 1024], P('pipe', 'dp')
- input_grads: bfloat16 [2, 8192, 1024], P('pipe', 'dp')
- grad_qkv: float32 [2, 1024, 3, 1024], P('pipe', None, None, 'tensor')
- grad_qv_bias: float32 [2, 2, 1024], P('pipe', None, 'tensor')
- grad_w_out: float32 [2, 1024, 1024], P('pipe', 'tensor')
- grad_out_bias: float32 [2, 1024], P('pipe')
- grad_w_up: float32 [2, 1024, 4096], P('pipe', None, 'tensor')
- grad_up_bias: float32 [2, 4096], P('pipe', 'tensor')
- grad_w_down: float32 [2, 4096, 1024], P('pipe', 'tensor')
- grad_down_bias: float32 [2, 1024], P('pipe')
- grad_gains: float32 [2, 2, 1024], P('pipe')
- grad_shifts: float32 [2, 2, 1024], P('pipe')
Inputs may be any that keep to these rules, and one draw needn't show every extreme that they name: `segment_ids`: ids never fall along the tokens; one document is 1 to 256 tokens.
All inputs are finite; a program needn't handle non-finite values.
Results may differ from a plain program's by a relative error of at most 0.035.
Values may be sent and summed in bfloat16 or wider, within the bound.
A program may use at most 128 MiB of HBM per device.

v0:
```python
import jax
import jax.numpy as jnp
from jax import lax
from jax.sharding import PartitionSpec as P

HEAD_DIM = 64
SEQ_LEN = 256
SEQ_MB = 1


NORM_EPS = 1e-05
GELU_COEF = 0.7978845608028654
CUBIC_COEF = 0.044715
MASKED_SCORE = -1e30


def passed_along(x, axis, by):
    peers = lax.axis_size(axis)
    pairs = [(i, i + by) for i in range(peers) if 0 <= i + by < peers]
    return lax.ppermute(x, axis, pairs)


def gelu_pair(pre_act):
    tanh_val = jnp.tanh(GELU_COEF * (pre_act + CUBIC_COEF * pre_act * pre_act * pre_act))
    gelu_value = 0.5 * pre_act * (1.0 + tanh_val)
    act_slope = 0.5 * (1.0 + tanh_val) + 0.5 * pre_act * (1.0 - tanh_val * tanh_val) * GELU_COEF * (
        1.0 + 3.0 * CUBIC_COEF * pre_act * pre_act
    )
    return (gelu_value, act_slope)


def layer_norm(rows_in, norm_gain, norm_shift):
    centred = rows_in - jnp.mean(rows_in, axis=-1, keepdims=True)
    inv_std = lax.rsqrt(jnp.mean(centred * centred, axis=-1, keepdims=True) + NORM_EPS)
    normed = centred * inv_std
    return (normed * norm_gain + norm_shift, normed, inv_std)


def norm_back(grad_out, normed, inv_std, norm_gain):
    scaled = grad_out * norm_gain
    return inv_std * (
        scaled
        - jnp.mean(scaled, axis=-1, keepdims=True)
        - normed * jnp.mean(scaled * normed, axis=-1, keepdims=True)
    )


def visible(seg_rows):
    length = seg_rows.shape[-1]
    position = jnp.arange(length)
    causal = position[:, None] >= position[None, :]
    same_doc = seg_rows[:, :, None] == seg_rows[:, None, :]
    return (causal[None] & same_doc)[:, None]


def scores_of(query_rows, key_rows, seg_rows):
    score_scale = query_rows.shape[-1] ** (-0.5)
    raw_scores = (
        jnp.einsum("sqhe,skhe->shqk", query_rows, key_rows, preferred_element_type=jnp.float32)
        * score_scale
    )
    return (jnp.where(visible(seg_rows), raw_scores, MASKED_SCORE), score_scale)


def attend(query_rows, key_rows, value_rows, seg_rows):
    scores, score_scale = scores_of(query_rows, key_rows, seg_rows)
    row_max = jnp.max(scores, axis=-1, keepdims=True)
    log_total = row_max + jnp.log(jnp.sum(jnp.exp(scores - row_max), axis=-1, keepdims=True))
    prob_rows = jnp.exp(scores - log_total).astype(jnp.bfloat16)
    mix_rows = jnp.einsum(
        "shqk,skhe->sqhe", prob_rows, value_rows, preferred_element_type=jnp.float32
    ).astype(jnp.bfloat16)
    return (mix_rows, log_total)


def attend_back(query_rows, key_rows, value_rows, seg_rows, log_total, grad_mix):
    scores, score_scale = scores_of(query_rows, key_rows, seg_rows)
    prob_rows = jnp.exp(scores - log_total)
    grad_prob = jnp.einsum(
        "sqhe,skhe->shqk", grad_mix, value_rows, preferred_element_type=jnp.float32
    )
    row_delta = jnp.sum(prob_rows * grad_prob, axis=-1, keepdims=True)
    grad_scores = (prob_rows * (grad_prob - row_delta) * score_scale).astype(jnp.bfloat16)
    g_query = jnp.einsum(
        "shqk,skhe->sqhe", grad_scores, key_rows, preferred_element_type=jnp.float32
    ).astype(jnp.bfloat16)
    g_key = jnp.einsum(
        "shqk,sqhe->skhe", grad_scores, query_rows, preferred_element_type=jnp.float32
    ).astype(jnp.bfloat16)
    g_value = jnp.einsum(
        "shqk,sqhe->skhe",
        prob_rows.astype(jnp.bfloat16),
        grad_mix,
        preferred_element_type=jnp.float32,
    ).astype(jnp.bfloat16)
    return (g_query, g_key, g_value)


def on_device(
    section_input,
    segment_ids,
    w_qkv,
    qv_bias,
    w_out,
    out_bias,
    w_up,
    up_bias,
    w_down,
    down_bias,
    norm_gains,
    norm_shifts,
    out_grad,
):
    section_index = lax.axis_index("pipe")
    is_first = section_index == 0
    proj_in = w_qkv[0]
    proj_out = w_out[0]
    up_proj = w_up[0]
    down_proj = w_down[0]
    out_shift = out_bias[0]
    up_shift = up_bias[0]
    down_shift = down_bias[0]
    norm_gain = norm_gains[0]
    norm_shift = norm_shifts[0]
    dmodel = proj_in.shape[0]
    columns = proj_in.shape[2]
    heads_here = columns // HEAD_DIM
    zero_row = jnp.zeros((1, columns), jnp.float32)
    qkv_shift = jnp.concatenate([qv_bias[0][0:1], zero_row, qv_bias[0][1:2]], axis=0)
    rows_mb = SEQ_MB * SEQ_LEN
    micro_count = section_input.shape[0] // rows_mb

    def combine(partial_rows):
        summed = lax.psum(partial_rows.astype(jnp.bfloat16), "tensor").astype(jnp.float32)
        return summed

    def batch_rows(source, batch_index):
        return lax.dynamic_slice_in_dim(source, batch_index * rows_mb, rows_mb, 0)

    incoming = jnp.zeros((rows_mb, dmodel), jnp.bfloat16)
    forward_outs = []
    states = []
    for tick_index in range(micro_count + 1):
        own_rows = batch_rows(section_input, min(tick_index, micro_count - 1))
        held_rows = jnp.where(is_first, own_rows, incoming)
        batch_here = jnp.clip(tick_index - section_index, 0, micro_count - 1)
        seg_rows = lax.dynamic_slice_in_dim(segment_ids, batch_here * rows_mb, rows_mb, 0).reshape(
            SEQ_MB, SEQ_LEN
        )
        residual = held_rows.astype(jnp.float32)
        first_norm, forward_normed1, forward_inv1 = layer_norm(
            residual, norm_gain[0], norm_shift[0]
        )
        forward_first_in = first_norm.astype(jnp.bfloat16)
        forward_qkv = (
            jnp.einsum("td,dgc->tgc", forward_first_in, proj_in, preferred_element_type=jnp.float32)
            + qkv_shift
        ).astype(jnp.bfloat16)
        forward_shaped = forward_qkv.reshape(SEQ_MB, SEQ_LEN, 3, heads_here, HEAD_DIM)
        mix_rows, forward_log_total = attend(
            forward_shaped[:, :, 0], forward_shaped[:, :, 1], forward_shaped[:, :, 2], seg_rows
        )
        forward_mix_flat = mix_rows.reshape(rows_mb, columns)
        middle = (
            residual
            + combine(jnp.dot(forward_mix_flat, proj_out, preferred_element_type=jnp.float32))
            + out_shift
        )
        second_norm, forward_normed2, forward_inv2 = layer_norm(middle, norm_gain[1], norm_shift[1])
        forward_second_in = second_norm.astype(jnp.bfloat16)
        pre_act = jnp.dot(forward_second_in, up_proj, preferred_element_type=jnp.float32) + up_shift
        gelu_value, forward_act_slope = gelu_pair(pre_act)
        forward_hidden = gelu_value.astype(jnp.bfloat16)
        result = (
            middle
            + combine(jnp.dot(forward_hidden, down_proj, preferred_element_type=jnp.float32))
            + down_shift
        ).astype(jnp.bfloat16)
        forward_kept_state = (
            forward_normed1,
            forward_inv1,
            forward_first_in,
            forward_qkv,
            forward_mix_flat,
            forward_log_total,
            forward_normed2,
            forward_inv2,
            forward_second_in,
            forward_act_slope,
            forward_hidden,
            seg_rows,
        )
        result, kept_state = (result, forward_kept_state)
        forward_outs.append(result)
        states.append(kept_state)
        incoming = passed_along(result, "pipe", 1)
    returning = jnp.zeros_like(incoming)
    back_outs = []
    grad_sums = None
    for tick_index in range(micro_count + 1):
        if tick_index < micro_count:
            own_grad = batch_rows(out_grad, micro_count - 1 - tick_index)
        else:
            own_grad = jnp.zeros_like(returning)
        cotangent = jnp.where(is_first, returning, own_grad)
        (
            normed1,
            inv1,
            first_in,
            qkv,
            mix_flat,
            log_total,
            normed2,
            inv2,
            second_in,
            act_slope,
            hidden,
            backward_seg_rows,
        ) = states[micro_count - tick_index]
        grad_top = cotangent.astype(jnp.float32)
        backward_g_down = jnp.einsum(
            "tf,td->fd", hidden, cotangent, preferred_element_type=jnp.float32
        )
        backward_g_down_shift = jnp.sum(grad_top, axis=0)
        g_hidden = jnp.einsum("td,fd->tf", cotangent, down_proj, preferred_element_type=jnp.float32)
        g_pre = (g_hidden * act_slope).astype(jnp.bfloat16)
        backward_g_up = jnp.einsum(
            "td,tf->df", second_in, g_pre, preferred_element_type=jnp.float32
        )
        backward_g_up_shift = jnp.sum(g_pre.astype(jnp.float32), axis=0)
        g_second = combine(
            jnp.einsum("tf,df->td", g_pre, up_proj, preferred_element_type=jnp.float32)
        )
        g_middle = grad_top + norm_back(g_second, normed2, inv2, norm_gain[1])
        g_gain2 = jnp.sum(g_second * normed2, axis=0)
        g_shift2 = jnp.sum(g_second, axis=0)
        middle_full = g_middle.astype(jnp.bfloat16)
        backward_g_proj_out = jnp.einsum(
            "tc,td->cd", mix_flat, middle_full, preferred_element_type=jnp.float32
        )
        backward_g_out_shift = jnp.sum(g_middle, axis=0)
        g_mix = jnp.einsum(
            "td,cd->tc", middle_full, proj_out, preferred_element_type=jnp.float32
        ).astype(jnp.bfloat16)
        shaped = qkv.reshape(SEQ_MB, SEQ_LEN, 3, heads_here, HEAD_DIM)
        g_query, g_key, g_value = attend_back(
            shaped[:, :, 0],
            shaped[:, :, 1],
            shaped[:, :, 2],
            backward_seg_rows,
            log_total,
            g_mix.reshape(SEQ_MB, SEQ_LEN, heads_here, HEAD_DIM),
        )
        g_qkv = jnp.stack([g_query, g_key, g_value], axis=2).reshape(rows_mb, 3, columns)
        backward_g_proj_in = jnp.einsum(
            "td,tgc->dgc", first_in, g_qkv, preferred_element_type=jnp.float32
        )
        qkv_sums = jnp.sum(g_qkv.astype(jnp.float32), axis=0)
        backward_g_qv = jnp.stack([qkv_sums[0], qkv_sums[2]], axis=0)
        g_first = combine(
            jnp.einsum("tgc,dgc->td", g_qkv, proj_in, preferred_element_type=jnp.float32)
        )
        g_gain1 = jnp.sum(g_first * normed1, axis=0)
        g_shift1 = jnp.sum(g_first, axis=0)
        g_low = (g_middle + norm_back(g_first, normed1, inv1, norm_gain[0])).astype(jnp.bfloat16)
        grads = (
            backward_g_proj_in,
            backward_g_qv,
            backward_g_proj_out,
            backward_g_out_shift,
            backward_g_up,
            backward_g_up_shift,
            backward_g_down,
            backward_g_down_shift,
            jnp.stack([g_gain1, g_gain2]),
            jnp.stack([g_shift1, g_shift2]),
        )
        g_low, grads = (g_low, grads)
        grad_sums = (
            grads
            if grad_sums is None
            else tuple((held + fresh for held, fresh in zip(grad_sums, grads)))
        )
        back_outs.append(g_low)
        returning = passed_along(g_low, "pipe", -1)
    out_list = [
        jnp.where(is_first, forward_outs[batch_index], forward_outs[batch_index + 1])
        for batch_index in range(micro_count)
    ]
    in_list = [
        jnp.where(
            is_first, back_outs[micro_count - batch_index], back_outs[micro_count - 1 - batch_index]
        )
        for batch_index in range(micro_count)
    ]
    (
        g_proj_in,
        g_qv,
        g_proj_out,
        g_out_shift,
        g_up,
        g_up_shift,
        g_down,
        g_down_shift,
        g_gains,
        g_shifts,
    ) = grad_sums
    out_full = jnp.concatenate(out_list, axis=0)
    in_full = jnp.concatenate(in_list, axis=0)
    (
        total_qkv,
        total_qv,
        total_out,
        total_up,
        total_up_shift,
        total_down,
        total_out_shift,
        total_down_shift,
        total_gains,
        total_shifts,
    ) = (
        lax.psum(g_proj_in.astype(jnp.bfloat16), "dp").astype(jnp.float32),
        lax.psum(g_qv.astype(jnp.bfloat16), "dp").astype(jnp.float32),
        lax.psum(g_proj_out.astype(jnp.bfloat16), "dp").astype(jnp.float32),
        lax.psum(g_up.astype(jnp.bfloat16), "dp").astype(jnp.float32),
        lax.psum(g_up_shift.astype(jnp.bfloat16), "dp").astype(jnp.float32),
        lax.psum(g_down.astype(jnp.bfloat16), "dp").astype(jnp.float32),
        lax.psum(g_out_shift.astype(jnp.bfloat16), "dp").astype(jnp.float32),
        lax.psum(g_down_shift.astype(jnp.bfloat16), "dp").astype(jnp.float32),
        lax.psum(g_gains.astype(jnp.bfloat16), "dp").astype(jnp.float32),
        lax.psum(g_shifts.astype(jnp.bfloat16), "dp").astype(jnp.float32),
    )
    return (
        out_full[None],
        in_full[None],
        total_qkv[None],
        total_qv[None],
        total_out[None],
        total_out_shift[None],
        total_up[None],
        total_up_shift[None],
        total_down[None],
        total_down_shift[None],
        total_gains[None],
        total_shifts[None],
    )


def solution(mesh):
    placed = (
        P("dp", None),
        P("dp"),
        P("pipe", None, None, "tensor"),
        P("pipe", None, "tensor"),
        P("pipe", "tensor", None),
        P("pipe", None),
        P("pipe", None, "tensor"),
        P("pipe", "tensor"),
        P("pipe", "tensor", None),
        P("pipe", None),
        P("pipe", None, None),
        P("pipe", None, None),
        P("dp", None),
    )
    return jax.shard_map(
        on_device,
        mesh=mesh,
        in_specs=placed,
        out_specs=(
            P("pipe", "dp", None),
            P("pipe", "dp", None),
            P("pipe", None, None, "tensor"),
            P("pipe", None, "tensor"),
            P("pipe", "tensor", None),
            P("pipe", None),
            P("pipe", None, "tensor"),
            P("pipe", "tensor"),
            P("pipe", "tensor", None),
            P("pipe", None),
            P("pipe", None, None),
            P("pipe", None, None),
        ),
        check_vma=False,
    )
```

profile of v0, /device:TPU:1, one launch (start us, length us, event | category | flops | bytes accessed | tf_op | source)
XLA Modules:
  0.0 1969.8 jit_solution(4981071526094199700)
XLA Ops:
  17.0 83.1 %all-reduce.24.cloned.1.call-done = bf16[256,1024]{1,0:T(8,128)(2,1)} async-done(((bf16[256,1024]{1,0:T(8,128)(2,1)}), bf16[256,1024]{1,0:T(8,128)(2,1)}) %all-reduce.24.cloned.1.call-update) | async-done | bytes 524304 | tf_op jit(solution)/shard_map/psum | solution.py:134
  107.1 83.5 %all-reduce.26.cloned.1.call-done = bf16[256,1024]{1,0:T(8,128)(2,1)} async-done(((bf16[256,1024]{1,0:T(8,128)(2,1)}), bf16[256,1024]{1,0:T(8,128)(2,1)}) %all-reduce.26.cloned.1.call-update) | async-done | bytes 524304 | tf_op jit(solution)/shard_map/psum | solution.py:134
  194.5 6.0 collective-permute-done
  205.5 85.9 %all-reduce.28.cloned.1.call-done = bf16[256,1024]{1,0:T(8,128)(2,1)} async-done(((bf16[256,1024]{1,0:T(8,128)(2,1)}), bf16[256,1024]{1,0:T(8,128)(2,1)}) %all-reduce.28.cloned.1.call-update) | async-done | bytes 524304 | tf_op jit(solution)/shard_map/psum | solution.py:134
  296.9 83.4 %all-reduce.30.cloned.1.call-done = bf16[256,1024]{1,0:T(8,128)(2,1)} async-done(((bf16[256,1024]{1,0:T(8,128)(2,1)}), bf16[256,1024]{1,0:T(8,128)(2,1)}) %all-reduce.30.cloned.1.call-update) | async-done | bytes 524304 | tf_op jit(solution)/shard_map/psum | solution.py:134
  385.0 6.0 collective-permute-done.1
  396.0 85.9 %all-reduce.32.cloned.1.call-done = bf16[256,1024]{1,0:T(8,128)(2,1)} async-done(((bf16[256,1024]{1,0:T(8,128)(2,1)}), bf16[256,1024]{1,0:T(8,128)(2,1)}) %all-reduce.32.cloned.1.call-update) | async-done | bytes 524304 | tf_op jit(solution)/shard_map/psum | solution.py:134
  488.6 83.5 %all-reduce.34.cloned.1.call-done = bf16[256,1024]{1,0:T(8,128)(2,1)} async-done(((bf16[256,1024]{1,0:T(8,128)(2,1)}), bf16[256,1024]{1,0:T(8,128)(2,1)}) %all-reduce.34.cloned.1.call-update) | async-done | bytes 524304 | tf_op jit(solution)/shard_map/psum | solution.py:134
  576.9 5.8 collective-permute-done.2
  587.7 85.9 %all-reduce.36.cloned.1.call-done = bf16[256,1024]{1,0:T(8,128)(2,1)} async-done(((bf16[256,1024]{1,0:T(8,128)(2,1)}), bf16[256,1024]{1,0:T(8,128)(2,1)}) %all-reduce.36.cloned.1.call-update) | async-done | bytes 524304 | tf_op jit(solution)/shard_map/psum | solution.py:134
  679.2 83.5 %all-reduce.38.cloned.1.call-done = bf16[256,1024]{1,0:T(8,128)(2,1)} async-done(((bf16[256,1024]{1,0:T(8,128)(2,1)}), bf16[256,1024]{1,0:T(8,128)(2,1)}) %all-reduce.38.cloned.1.call-update) | async-done | bytes 524304 | tf_op jit(solution)/shard_map/psum | solution.py:134
  767.3 6.0 collective-permute-done.3
  778.8 85.9 %all-reduce.40.cloned.1.call-done = bf16[256,1024]{1,0:T(8,128)(2,1)} async-done(((bf16[256,1024]{1,0:T(8,128)(2,1)}), bf16[256,1024]{1,0:T(8,128)(2,1)}) %all-reduce.40.cloned.1.call-update) | async-done | bytes 524304 | tf_op jit(solution)/shard_map/psum | solution.py:134
  872.6 83.4 %all-reduce.42.cloned.1.call-done = bf16[256,1024]{1,0:T(8,128)(2,1)} async-done(((bf16[256,1024]{1,0:T(8,128)(2,1)}), bf16[256,1024]{1,0:T(8,128)(2,1)}) %all-reduce.42.cloned.1.call-update) | async-done | bytes 524304 | tf_op jit(solution)/shard_map/psum | solution.py:134
  975.7 83.5 %all-reduce.44.cloned.1.call-done = bf16[256,1024]{1,0:T(8,128)(2,1)} async-done(((bf16[256,1024]{1,0:T(8,128)(2,1)}), bf16[256,1024]{1,0:T(8,128)(2,1)}) %all-reduce.44.cloned.1.call-update) | async-done | bytes 524304 | tf_op jit(solution)/shard_map/psum | solution.py:134
  1067.1 6.4 collective-permute-done.4
  1077.8 3.2 fusion.314
  1082.9 79.4 %all-reduce.46.cloned.1.call-done = bf16[256,1024]{1,0:T(8,128)(2,1)} async-done(((bf16[256,1024]{1,0:T(8,128)(2,1)}), bf16[256,1024]{1,0:T(8,128)(2,1)}) %all-reduce.46.cloned.1.call-update) | async-done | bytes 524304 | tf_op jit(solution)/shard_map/psum | solution.py:134
  1171.1 2.6 convolution_convert_fusion.31
  1173.8 2.7 convolution_convert_fusion.30
  1187.9 2.7 fusion.241
  1190.6 78.5 %all-reduce.48.cloned.1.call-done = bf16[256,1024]{1,0:T(8,128)(2,1)} async-done(((bf16[256,1024]{1,0:T(8,128)(2,1)}), bf16[256,1024]{1,0:T(8,128)(2,1)}) %all-reduce.48.cloned.1.call-update) | async-done | bytes 524304 | tf_op jit(solution)/shard_map/psum | solution.py:134
  1271.3 2.8 broadcast_select_fusion
  1280.1 4.1 collective-permute-done.5
  1289.8 2.7 fusion.239
  1293.6 80.4 %all-reduce.50.cloned.1.call-done = bf16[256,1024]{1,0:T(8,128)(2,1)} async-done(((bf16[256,1024]{1,0:T(8,128)(2,1)}), bf16[256,1024]{1,0:T(8,128)(2,1)}) %all-reduce.50.cloned.1.call-update) | async-done | bytes 524304 | tf_op jit(solution)/shard_map/psum | solution.py:134
  1383.7 2.7 convolution_convert_fusion.27
  1394.4 3.0 fusion.393
  1397.5 79.1 %all-reduce.52.cloned.1.call-done = bf16[256,1024]{1,0:T(8,128)(2,1)} async-done(((bf16[256,1024]{1,0:T(8,128)(2,1)}), bf16[256,1024]{1,0:T(8,128)(2,1)}) %all-reduce.52.cloned.1.call-update) | async-done | bytes 524304 | tf_op jit(solution)/shard_map/psum | solution.py:134
  1478.7 2.8 broadcast_select_fusion.1
  1487.3 4.3 collective-permute-done.6
  1497.3 2.9 fusion.392
  1500.2 81.2 %all-reduce.54.cloned.1.call-done = bf16[256,1024]{1,0:T(8,128)(2,1)} async-done(((bf16[256,1024]{1,0:T(8,128)(2,1)}), bf16[256,1024]{1,0:T(8,128)(2,1)}) %all-reduce.54.cloned.1.call-update) | async-done | bytes 524304 | tf_op jit(solution)/shard_map/psum | solution.py:134
  1583.8 2.6 fusion.399
  1595.7 3.1 fusion.374
  1599.3 79.6 %all-reduce.56.cloned.1.call-done = bf16[256,1024]{1,0:T(8,128)(2,1)} async-done(((bf16[256,1024]{1,0:T(8,128)(2,1)}), bf16[256,1024]{1,0:T(8,128)(2,1)}) %all-reduce.56.cloned.1.call-update) | async-done | bytes 524304 | tf_op jit(solution)/shard_map/psum | solution.py:134
  1681.1 2.8 broadcast_select_fusion.2
  1688.2 5.8 collective-permute-done.7
  1696.9 5.6 fusion.166
  1703.6 2.9 fusion.35
  1706.5 74.3 %all-reduce.58.cloned.1.call-done = bf16[256,1024]{1,0:T(8,128)(2,1)} async-done(((bf16[256,1024]{1,0:T(8,128)(2,1)}), bf16[256,1024]{1,0:T(8,128)(2,1)}) %all-reduce.58.cloned.1.call-update) | async-done | bytes 524304 | tf_op jit(solution)/shard_map/psum | solution.py:134
  1783.3 2.7 fusion.400
  1799.7 3.8 fusion.36
  1804.2 78.1 %all-reduce.62.cloned.1.call-done = (bf16[256,1024]{1,0:T(8,128)(2,1)}, bf16[256,1024]{1,0:T(8,128)(2,1)}) async-done(((bf16[256,1024]{1,0:T(8,128)(2,1)}, bf16[256,1024]{1,0:T(8,128)(2,1)}), (bf16[256,1024]{1,0:T(8,128)(2,1)}, bf16[256,1024]{1,0:T(8,128)(2,1)})) %all-reduce.62.cloned.1.call-update) | async-done | bytes 1048592 | tf_op jit(solution)/shard_map/psum | solution.py:134
  1884.4 26.1 %all-reduce = (bf16[1,2,128]{2,1,0:T(2,128)(2,1)S(1)}, bf16[1,1024]{1,0:T(2,128)(2,1)S(1)}, bf16[1,512]{1,0:T(2,128)(2,1)S(1)}, bf16[1,1024]{1,0:T(2,128)(2,1)S(...) all-reduce(bf16[1,2,128]{2,1,0:T(2,128)(2,1)S(1)} %fusion.354, ...), channel_id=1, replica_groups=mesh['pipe'=2,'tensor'=8,'dp'=8] {'dp'}, use_global_device_ids=true, to_apply=%region_81.82 | all-reduce | flops 6912 | bytes 27648 | tf_op jit(solution)/shard_map/psum | solution.py:323
  1914.1 2.6 fusion.232
  1920.2 35.9 %all-reduce.60.cloned.1.call-done = (bf16[1,1024,3,128]{3,1,2,0:T(8,128)(2,1)}, bf16[1,128,1024]{2,1,0:T(8,128)(2,1)}, bf16[1,1024,512]{2,1,0:T(8,128)(2,1)}, bf16[1,512,1024]{2,1,0:T(8,128)(2,1)}) async-done(((bf16[1,1024,3,128]{3,1,2,0:T(8,128)(2,1)}, bf16[1,128,1024]{2,1,0:T(8,128)(2,1)}, bf16[1,1024,512]{2,1,0:T(8,128)(2,1)}, bf16[1,512,1024]{2,1,0:T(8,128)(2,1)}), (bf16[1,1024,3,128]{3,1,2,0:T(8,128)(2,1)}, ...) | async-done | bytes 3145744 | tf_op jit(solution)/shard_map/psum | solution.py:322
  1956.2 2.9 broadcast_in_dim.243
  (680 shorter events, 231.4 us)
Async XLA Ops:
  7.2 98.5 %copy-start = (bf16[1,512,1024]{2,1,0:T(8,128)(2,1)S(1)}, bf16[1,512,1024]{2,1,0:T(8,128)(2,1)}, u32[]{:S(2)}) copy-start(bf16[1,512,1024]{2,1,0:T(8,128)(2,1)} %param.21) | copy-start | bytes 3145732
  7.2 92.9 %all-reduce.24.cloned.1.call-start = ((), (), s32[]{:S(2)}) async-start(), calls=%async_computation | async-start | bytes 1048576 | tf_op jit(solution)/shard_map/psum | solution.py:134
  11.5 763.4 %copy-start.146 = (f32[1,1,1024]{2,1,0:T(1,128)}, f32[1,1,1024]{2,1,0:T(1,128)S(1)}, u32[]{:S(2)}) copy-start(f32[1,1,1024]{2,1,0:T(1,128)S(1)} %get-tuple-element.104) | copy-start | bytes 12292
  15.0 85.2 %copy-start.47 = (f32[1,1024]{1,0:T(1,128)S(1)}, f32[1,1024]{1,0:T(1,128)}, u32[]{:S(2)}) copy-start(f32[1,1024]{1,0:T(1,128)} %param.18) | copy-start | bytes 12292
  15.1 86.5 %copy-start.96 = (bf16[256,3,128]{0,2,1:T(8,128)(2,1)}, bf16[256,3,128]{0,2,1:T(8,128)(2,1)S(1)}, u32[]{:S(2)}) copy-start(bf16[256,3,128]{0,2,1:T(8,128)(2,1)S(1)} %add_convert_fusion.17) | copy-start | bytes 589828
  15.5 87.8 %copy-start.2 = (bf16[1,1024,512]{2,1,0:T(8,128)(2,1)S(1)}, bf16[1,1024,512]{2,1,0:T(8,128)(2,1)}, u32[]{:S(2)}) copy-start(bf16[1,1024,512]{2,1,0:T(8,128)(2,1)} %param.19) | copy-start | bytes 3145732
  15.5 87.8 %copy-start.200 = (f32[1,512]{1,0:T(1,128)S(1)}, f32[1,512]{1,0:T(1,128)}, u32[]{:S(2)}) copy-start(f32[1,512]{1,0:T(1,128)} %param.20) | copy-start | bytes 6148
  15.5 84.6 %copy-start.130 = (f32[2,256]{1,0:T(2,128)}, f32[2,256]{1,0:T(2,128)S(1)}, u32[]{:S(2)}) copy-start(f32[2,256]{1,0:T(2,128)S(1)} %log_add_fusion.4) | copy-start | bytes 6148
  15.8 89.1 %copy-start.87 = (bf16[2,64,256]{2,1,0:T(8,128)(2,1)}, bf16[2,64,256]{2,1,0:T(8,128)(2,1)S(1)}, u32[]{:S(2)}) copy-start(bf16[2,64,256]{2,1,0:T(8,128)(2,1)S(1)} %convolution_convert_fusion.39) | copy-start | bytes 196612
  16.9 173.6 %all-reduce.26.cloned.1.call-start = ((), (), s32[]{:S(2)}) async-start(), calls=%async_computation.1 | async-start | bytes 1048576 | tf_op jit(solution)/shard_map/psum | solution.py:134
  105.7 84.8 %copy-start.116 = (f32[1,1024]{1,0:T(1,128)S(1)}, f32[1,1024]{1,0:T(1,128)}, u32[]{:S(2)}) copy-start(f32[1,1024]{1,0:T(1,128)} %param.22) | copy-start | bytes 12292
  107.0 184.3 %all-reduce.28.cloned.1.call-start = ((), (), s32[]{:S(2)}) async-start(), calls=%async_computation.2 | async-start | bytes 1048576 | tf_op jit(solution)/shard_map/psum | solution.py:134
  192.1 8.3 collective-permute-start
  203.4 88.0 %copy-start.132 = (f32[2,256]{1,0:T(2,128)}, f32[2,256]{1,0:T(2,128)S(1)}, u32[]{:S(2)}) copy-start(f32[2,256]{1,0:T(2,128)S(1)} %log_add_fusion.3) | copy-start | bytes 6148
  205.4 174.9 %all-reduce.30.cloned.1.call-start = ((), (), s32[]{:S(2)}) async-start(), calls=%async_computation.3 | async-start | bytes 1048576 | tf_op jit(solution)/shard_map/psum | solution.py:134
  295.5 84.8 %copy-start.53 = (bf16[256,1024]{1,0:T(8,128)(2,1)S(1)}, bf16[256,1024]{1,0:T(8,128)(2,1)}, u32[]{:S(2)}) copy-start(bf16[256,1024]{1,0:T(8,128)(2,1)} %copy-done.52) | copy-start | bytes 1572868
  296.8 185.0 %all-reduce.32.cloned.1.call-start = ((), (), s32[]{:S(2)}) async-start(), calls=%async_computation.4 | async-start | bytes 1048576 | tf_op jit(solution)/shard_map/psum | solution.py:134
  382.7 8.3 collective-permute-start.1
  393.9 87.9 %copy-start.134 = (f32[2,256]{1,0:T(2,128)}, f32[2,256]{1,0:T(2,128)S(1)}, u32[]{:S(2)}) copy-start(f32[2,256]{1,0:T(2,128)S(1)} %log_add_fusion.2) | copy-start | bytes 6148
  395.9 176.2 %all-reduce.34.cloned.1.call-start = ((), (), s32[]{:S(2)}) async-start(), calls=%async_computation.5 | async-start | bytes 1048576 | tf_op jit(solution)/shard_map/psum | solution.py:134
  488.5 185.1 %all-reduce.36.cloned.1.call-start = ((), (), s32[]{:S(2)}) async-start(), calls=%async_computation.6 | async-start | bytes 1048576 | tf_op jit(solution)/shard_map/psum | solution.py:134
  574.4 8.3 collective-permute-start.2
  585.7 88.0 %copy-start.135 = (f32[2,256]{1,0:T(2,128)}, f32[2,256]{1,0:T(2,128)S(1)}, u32[]{:S(2)}) copy-start(f32[2,256]{1,0:T(2,128)S(1)} %log_add_fusion.1) | copy-start | bytes 6148
  587.7 175.0 %all-reduce.38.cloned.1.call-start = ((), (), s32[]{:S(2)}) async-start(), calls=%async_computation.7 | async-start | bytes 1048576 | tf_op jit(solution)/shard_map/psum | solution.py:134
  679.1 185.6 %all-reduce.40.cloned.1.call-start = ((), (), s32[]{:S(2)}) async-start(), calls=%async_computation.8 | async-start | bytes 1048576 | tf_op jit(solution)/shard_map/psum | solution.py:134
  765.2 8.2 collective-permute-start.3
  776.7 88.0 %copy-start.136 = (f32[2,256]{1,0:T(2,128)}, f32[2,256]{1,0:T(2,128)S(1)}, u32[]{:S(2)}) copy-start(f32[2,256]{1,0:T(2,128)S(1)} %log_add_fusion) | copy-start | bytes 6148
  778.7 177.3 %all-reduce.42.cloned.1.call-start = ((), (), s32[]{:S(2)}) async-start(), calls=%async_computation.9 | async-start | bytes 1048576 | tf_op jit(solution)/shard_map/psum | solution.py:134
  866.1 92.3 %copy-start.124 = (f32[256]{0:T(256)}, f32[256]{0:T(256)S(1)}, u32[]{:S(2)}) copy-start(f32[256]{0:T(256)S(1)} %broadcast_multiply_fusion.20) | copy-start | bytes 3076
  867.5 90.9 %copy-start.144 = (f32[256]{0:T(256)}, f32[256]{0:T(256)S(1)}, u32[]{:S(2)}) copy-start(f32[256]{0:T(256)S(1)} %add_rsqrt_fusion) | copy-start | bytes 3076
  872.5 186.6 %all-reduce.44.cloned.1.call-start = ((), (), s32[]{:S(2)}) async-start(), calls=%async_computation.10 | async-start | bytes 1048576 | tf_op jit(solution)/shard_map/psum | solution.py:134
  975.6 186.7 %all-reduce.46.cloned.1.call-start = ((), (), s32[]{:S(2)}) async-start(), calls=%async_computation.11 | async-start | bytes 1048576 | tf_op jit(solution)/shard_map/psum | solution.py:134
  1063.3 10.2 collective-permute-start.4
  1077.7 191.4 %all-reduce.48.cloned.1.call-start = ((), (), s32[]{:S(2)}) async-start(), calls=%async_computation.12 | async-start | bytes 1048576 | tf_op jit(solution)/shard_map/psum | solution.py:134
  1185.5 188.5 %all-reduce.50.cloned.1.call-start = ((), (), s32[]{:S(2)}) async-start(), calls=%async_computation.13 | async-start | bytes 1048576 | tf_op jit(solution)/shard_map/psum | solution.py:134
  1274.1 10.1 collective-permute-start.5
  1289.3 187.2 %all-reduce.52.cloned.1.call-start = ((), (), s32[]{:S(2)}) async-start(), calls=%async_computation.14 | async-start | bytes 1048576 | tf_op jit(solution)/shard_map/psum | solution.py:134
  1393.0 188.4 %all-reduce.54.cloned.1.call-start = ((), (), s32[]{:S(2)}) async-start(), calls=%async_computation.15 | async-start | bytes 1048576 | tf_op jit(solution)/shard_map/psum | solution.py:134
  1481.5 10.1 collective-permute-start.6
  1496.7 182.2 %all-reduce.56.cloned.1.call-start = ((), (), s32[]{:S(2)}) async-start(), calls=%async_computation.16 | async-start | bytes 1048576 | tf_op jit(solution)/shard_map/psum | solution.py:134
  1500.2 87.2 %copy-start.10 = (bf16[1,128,1024]{2,1,0:T(8,128)(2,1)S(1)}, bf16[1,128,1024]{2,1,0:T(8,128)(2,1)}, u32[]{:S(2)}) copy-start(bf16[1,128,1024]{2,1,0:T(8,128)(2,1)} %param.17) | copy-start | bytes 786436
  1595.4 185.4 %all-reduce.58.cloned.1.call-start = ((), (), s32[]{:S(2)}) async-start(), calls=%async_computation.17 | async-start | bytes 1048576 | tf_op jit(solution)/shard_map/psum | solution.py:134
  1683.9 10.0 collective-permute-start.7
  1696.1 186.2 %all-reduce.62.cloned.1.call-start = ((), (), s32[]{:S(2)}) async-start(), calls=%async_computation.19 | async-start | bytes 2097152 | tf_op jit(solution)/shard_map/psum | solution.py:134
  1795.9 160.3 %all-reduce.60.cloned.1.call-start = ((), (), s32[]{:S(2)}) async-start(), calls=%async_computation.18 | async-start | bytes 6291456 | tf_op jit(solution)/shard_map/psum | solution.py:322
  1803.7 110.3 %copy-start.13 = (bf16[256,1024]{1,0:T(8,128)(2,1)S(1)}, bf16[256,1024]{1,0:T(8,128)(2,1)}, u32[]{:S(2)}) copy-start(bf16[256,1024]{1,0:T(8,128)(2,1)} %all-reduce.40.cloned.1.call-done) | copy-start | bytes 1572868
  1803.8 110.3 %copy-start.30 = (f32[256,1024]{1,0:T(8,128)S(1)}, f32[256,1024]{1,0:T(8,128)}, u32[]{:S(2)}) copy-start(f32[256,1024]{1,0:T(8,128)} %copy-done.29) | copy-start | bytes 3145732
  1803.8 110.3 %copy-start.117 = (f32[1,1024]{1,0:T(1,128)S(1)}, f32[1,1024]{1,0:T(1,128)}, u32[]{:S(2)}) copy-start(f32[1,1024]{1,0:T(1,128)} %param.22) | copy-start | bytes 12292
  (181 other events, 2480.2 us)
Sparse Core Ops, SparseCore 0:
  17.0 83.0 all-reduce.23
  107.2 83.3 all-reduce.25
  205.5 85.8 all-reduce.27
  296.9 83.3 all-reduce.29
  396.0 85.7 all-reduce.31
  488.6 83.3 all-reduce.33
  587.8 85.8 all-reduce.35
  679.2 83.3 all-reduce.37
  778.8 85.8 all-reduce.39
  872.7 83.3 all-reduce.41
  975.7 83.3 all-reduce.43
  1077.8 84.4 all-reduce.45
  1185.7 83.3 all-reduce.47
  1289.4 84.5 all-reduce.49
  1393.2 83.3 all-reduce.51
  1496.8 84.5 all-reduce.53
  1595.6 83.2 all-reduce.55
  1696.2 84.5 all-reduce.57
  1796.0 86.2 all-reduce.61
  1885.4 70.7 all-reduce.59
where the time goes:
time: 1980 us; the launch traced here: 1970 us
  waiting for transfers between devices  1640 us (83%)
  matrix products  134 us (7%)
  other arithmetic  103 us (5%)
  local copies, waits for them, and re-layouts  35.6 us (2%)
  blocking collectives  26.1 us (1%)
    psum x19, waiting for transfers between devices, combine(): lax.psum(partial_rows.astype(jnp.bfloat16), 'tensor').astype(jnp.float32)  1560 us
    ppermute x8, waiting for transfers between devices, passed_along(): return lax.ppermute(x, axis, pairs)  44.3 us
  transfers between devices with their start and end apart: 28, of which 28 were waited for; matrix products, arithmetic and copies ran while one was open for 3% of the time, Pallas kernels for 0%

commit v1 on v0

v1 whole, which is shorter than its diff:
```python
import jax
import jax.numpy as jnp
from jax import lax
from jax.experimental import pallas as pl
from jax.experimental.pallas import tpu as pltpu
from jax.sharding import PartitionSpec as P

MESH = pl.DeviceIdType.MESH
F32 = jnp.float32
BF16 = jnp.bfloat16

SEQ = 256
D = 1024
R = 64
NORM_EPS = 1e-05
GELU_COEF = 0.7978845608028654
CUBIC_COEF = 0.044715
MASKED_SCORE = -1e30
SCALE = 0.125
WQ, WO, WU, WD = range(4)
ROWS = (1024, 128, 1024, 512)
COLS = (384, 1024, 512, 1024)


def dot_nn(a, b):
    return jnp.dot(a, b, preferred_element_type=F32)


def dot_nt(a, b):
    return lax.dot_general(a, b, (((1,), (1,)), ((), ())), preferred_element_type=F32)


def dot_tn(a, b):
    return lax.dot_general(a, b, (((0,), (0,)), ((), ())), preferred_element_type=F32)


def loop(n, body):
    lax.fori_loop(0, n, lambda i, c: (body(i), c)[1], 0)


def ds(start, size):
    return pl.ds(pl.multiple_of(start, size), size)


def norm(rows):
    centred = rows - jnp.mean(rows, axis=-1, keepdims=True)
    inv = lax.rsqrt(jnp.mean(centred * centred, axis=-1, keepdims=True) + NORM_EPS)
    return centred * inv, inv


def norm_back(grad, normed, inv, gain):
    e = grad * gain
    return inv * (
        e - jnp.mean(e, axis=-1, keepdims=True) - normed * jnp.mean(e * normed, axis=-1, keepdims=True)
    )


def kernel(
    x_in, seg_in, wq_in, qvb_in, wo_in, outb_in, wu_in, upb_in, wd_in, downb_in, gain_in, shift_in, og_in,
    so_out, ig_out, gq_out, go_out, gu_out, gd_out, small_out, up_out, qv_out,
    wq, wo, wu, wd, prm, mask, xs_buf, g_buf, a1, a2, dyb, xo, ig0, qkv, prob, mix, hid, slope, du, dqkv, acc,
    rs_out, rs_in, n1, n2, i1, i2, yrow, dyrow,
    gq, go, gu, gd, cq, co, cu, cd, yq, yo, yu, yd, zq, zo, zu, zd, sm, sm2, sm3, smy, smz, smx,
    x_s, x_r, wy_s, wy_r, wc_s, wc_r, pr_s, pr_r, loc, gc_s, gc_r, gy_s, gy_r, gz_s, gz_r, ga_s, ga_r, gl,
    sm_s, sm_r, o_s, o_r, o_l,
):
    p = lax.axis_index("pipe")
    t = lax.axis_index("tensor")
    dp = lax.axis_index("dp")
    h_me, x = lax.div(t, 4), lax.rem(t, 4)
    z, c = lax.div(dp, 2), lax.rem(dp, 2)
    y = h_me * 2 + p

    def dev(xx, yy, zz, cc):
        return {"pipe": lax.rem(yy, 2), "tensor": lax.div(yy, 2) * 4 + xx, "dp": zz * 2 + cc}

    def xp(d):
        return lax.rem(x + d, 4)

    def yp(d):
        return lax.rem(y + d, 4)

    def zp(d):
        return lax.rem(z + d, 4)

    core_peer = dev(x, y, z, 1 - c)

    def remote(src, dst, ss, rs, device):
        return pltpu.make_async_remote_copy(
            src_ref=src, dst_ref=dst, send_sem=ss, recv_sem=rs, device_id=device, device_id_type=MESH
        )

    own = ds(x * R, R)
    w_in = (wq_in, wo_in, wu_in, wd_in)
    w_all = (wq, wo, wu, wd)
    g_all = (gq, go, gu, gd)
    c_all = (cq, co, cu, cd)
    y_all = (yq, yo, yu, yd)
    z_all = (zq, zo, zu, zd)
    g_outs = (gq_out, go_out, gu_out, gd_out)

    zc_peers = [(dz, dc) for dz in range(4) for dc in range(2) if (dz, dc) != (0, 0)]

    barrier = pltpu.get_barrier_semaphore()
    peers = [dev(xp(d), y, z, c) for d in (1, 2, 3)]
    peers += [dev(x, yp(d), z, c) for d in (1, 2, 3)]
    peers += [dev(x, y, zp(dz), lax.rem(c + dc, 2)) for dz, dc in zc_peers]
    for peer in peers:
        pl.semaphore_signal(barrier, inc=1, device_id=peer, device_id_type=MESH)

    load_x = pltpu.make_async_copy(x_in.at[ds(y * SEQ, SEQ)], xs_buf.at[0], loc.at[0])
    load_g = pltpu.make_async_copy(og_in.at[ds(y * SEQ, SEQ)], g_buf.at[1], loc.at[1])
    load_x.start()
    load_g.start()
    load_w = [pltpu.make_async_copy(w_in[k], w_all[k].at[y], loc.at[2 + k]) for k in range(4)]
    for copy in load_w:
        copy.start()

    prm[y] = jnp.zeros((8, D), F32)
    prm[y, 0:1, :] = outb_in[...]
    prm[y, 1:2, :] = downb_in[...]
    prm[y, 2:4, :] = gain_in[...]
    prm[y, 4:6, :] = shift_in[...]
    prm[y, 6:7, 0:512] = upb_in[...]
    prm[y, 7:8, 0:128] = qvb_in[0:1, :]
    prm[y, 7:8, 128:256] = qvb_in[1:2, :]
    sm[...] = jnp.zeros_like(sm)

    pl.semaphore_wait(barrier, len(peers))

    def send_prm(d):
        return remote(prm.at[y], prm.at[y], pr_s.at[d - 1], pr_r.at[d - 1], dev(x, yp(d), z, c))

    for d in (1, 2, 3):
        send_prm(d).start()

    def half_rows(k, which):
        return ds(which * (ROWS[k] // 2), ROWS[k] // 2)

    def w_send(k, d):
        rows = half_rows(k, c)
        i = k * 3 + d - 1
        return remote(w_in[k].at[rows], w_all[k].at[y, rows], wy_s.at[i], wy_r.at[i], dev(x, yp(d), z, c))

    def w_pass(k, d):
        rows = half_rows(k, c)
        i = k * 3 + d - 1
        block = w_all[k].at[lax.rem(y - d + 4, 4), rows]
        return remote(block, block, wc_s.at[i], wc_r.at[i], core_peer)

    def w_send_all(s):
        @pl.when(p == s)
        def _():
            for k in range(4):
                for d in (2, 1, 3):
                    w_send(k, d).start()

    def w_forward(s, k):
        @pl.when(p == s)
        def _():
            w_send(k, 2).wait_recv()
            w_pass(k, 2).start()

        @pl.when(p != s)
        def _():
            for d in (1, 3):
                w_send(k, d).wait_recv()
                w_pass(k, d).start()

    def w_ready(s, k):
        @pl.when(p == s)
        def _():
            load_w[k].wait()
            w_pass(k, 2).wait_recv()

        @pl.when(p != s)
        def _():
            for d in (1, 3):
                w_pass(k, d).wait_recv()

    def rs_copy(k, d):
        dest = xp(d)
        return remote(
            rs_out.at[k // 2, ds(dest * R, R)], rs_in.at[k // 2, d - 1], x_s.at[k * 3 + d - 1], x_r.at[k * 3 + d - 1],
            dev(dest, y, z, c),
        )

    def rs_start(k):
        for d in (2, 1, 3):
            rs_copy(k, d).start()

    def rs_finish(k):
        total = acc[own, :]
        for d in (1, 3, 2):
            rs_copy(k, d).wait_recv()
            total = total + rs_in[k // 2, d - 1].astype(F32)
        return total

    def ag_copy(k, ref, d):
        return remote(ref.at[own], ref.at[own], x_s.at[k * 3 + d - 1], x_r.at[k * 3 + d - 1], dev(xp(d), y, z, c))

    def ag_start(k, ref):
        for d in (2, 1, 3):
            ag_copy(k, ref, d).start()

    def ag_finish(k, ref):
        for d in (1, 3, 2):
            ag_copy(k, ref, d).wait_recv()

    def out_copy(i, ref, out, d):
        rows = ds(y * SEQ, SEQ)
        j = i * 3 + d - 1
        return remote(ref, out.at[rows], o_s.at[j], o_r.at[j], dev(x, yp(d), z, c))

    def out_local(i, ref, out):
        return pltpu.make_async_copy(ref, out.at[ds(y * SEQ, SEQ)], o_l.at[i])

    def out_start(i, s, ref, out):
        for d in (1, 2, 3):
            @pl.when(lax.rem(y + d, 2) == s)
            def _():
                out_copy(i, ref, out, d).start()

        @pl.when(p == s)
        def _():
            out_local(i, ref, out).start()

    def out_finish(i, s, ref, out):
        for d in (1, 2, 3):
            @pl.when(lax.rem(y + d, 2) == s)
            def _():
                out_copy(i, ref, out, d).wait_send()

        @pl.when(p == s)
        def _():
            out_local(i, ref, out).wait()
            for d in (1, 2, 3):
                out_copy(i, ref, out, d).wait_recv()

    def gc_copy(s, k, h):
        i = (s * 4 + k) * 2 + h
        return remote(g_all[k].at[s, h, half_rows(k, 1 - c)], c_all[k].at[s, h], gc_s.at[i], gc_r.at[i], core_peer)

    def gc_start(s, k):
        for h in (0, 1):
            gc_copy(s, k, h).start()

    def sum_rows(k, target, base, sources, rows):
        step = min(rows, 64)

        def body(r):
            here = pl.ds(pl.multiple_of(base + r * step, 16), step)
            there = pl.ds(pl.multiple_of(r * step, 16), step)
            total = target[here, :].astype(F32)
            for source in sources:
                total = total + source[there, :].astype(F32)
            target[here, :] = total.astype(BF16)

        loop(rows // step, body)

    def gy_copy(s, k, h):
        d = lax.rem(2 * h + s - y + 4, 4)
        i = (s * 4 + k) * 2 + h
        return remote(
            g_all[k].at[s, h, half_rows(k, c)], y_all[k].at[d - 1], gy_s.at[i], gy_r.at[k * 3 + d - 1],
            dev(x, 2 * h + s, z, c),
        )

    def gy_start(s, k):
        for h in (0, 1):
            gc_copy(s, k, h).wait_recv()
            sum_rows(k, g_all[k].at[s, h], c * (ROWS[k] // 2), [c_all[k].at[s, h]], ROWS[k] // 2)

            @pl.when(y != 2 * h + s)
            def _():
                gy_copy(s, k, h).start()

    def piece(k, zz):
        q = ROWS[k] // 8
        return pl.ds(pl.multiple_of(c * (ROWS[k] // 2) + zz * q, 16), q)

    def gz_copy(s, k, d):
        zz = zp(d)
        i = k * 3 + d - 1
        return remote(
            g_all[k].at[s, h_me, piece(k, zz)], z_all[k].at[d - 1], gz_s.at[i], gz_r.at[i], dev(x, y, zz, c)
        )

    def gz_start(s, k):
        @pl.when(p == s)
        def _():
            for d in (1, 2, 3):
                slot = y_all[k].at[d - 1]
                remote(slot, slot, gy_s.at[0], gy_r.at[k * 3 + d - 1], dev(x, yp(d), z, c)).wait_recv()
            sum_rows(
                k, g_all[k].at[s, h_me], c * (ROWS[k] // 2), [y_all[k].at[j] for j in range(3)], ROWS[k] // 2
            )
            for d in (2, 1, 3):
                gz_copy(s, k, d).start()

    def ga_copy(s, k, j):
        dz, dc = zc_peers[j]
        i = k * 7 + j
        rows = piece(k, z)
        return remote(
            g_all[k].at[s, h_me, rows], g_outs[k].at[rows], ga_s.at[i], ga_r.at[i],
            dev(x, y, zp(dz), lax.rem(c + dc, 2)),
        )

    def ga_local(s, k):
        rows = piece(k, z)
        return pltpu.make_async_copy(g_all[k].at[s, h_me, rows], g_outs[k].at[rows], gl.at[k])

    def ga_start(s, k):
        @pl.when(p == s)
        def _():
            q = ROWS[k] // 8
            for d in (1, 3, 2):
                gz_copy(s, k, d).wait_recv()
            sum_rows(
                k, g_all[k].at[s, h_me], c * (ROWS[k] // 2) + z * q, [z_all[k].at[j] for j in range(3)], q
            )
            for j in range(7):
                ga_copy(s, k, j).start()
            ga_local(s, k).start()

    def ga_finish(s, k):
        @pl.when(p == s)
        def _():
            ga_local(s, k).wait()
            for j in range(7):
                ga_copy(s, k, j).wait_recv()

    w_send_all(0)

    seg = seg_in[pl.ds(y, 1), :].astype(F32)
    seg_b = jnp.broadcast_to(seg, (SEQ, SEQ))
    rows_i = lax.broadcasted_iota(jnp.int32, (SEQ, SEQ), 0)
    cols_i = lax.broadcasted_iota(jnp.int32, (SEQ, SEQ), 1)
    mask[...] = jnp.where((rows_i >= cols_i) & (seg_b == seg_b.T), 0.0, MASKED_SCORE)

    low_lanes = lax.broadcasted_iota(jnp.int32, (SEQ, 128), 1) < 64

    def pick_head(value, e):
        keep = low_lanes if e == 0 else jnp.logical_not(low_lanes)
        return jnp.where(keep, value, jnp.zeros_like(value))

    def first_norm(s):
        def body(r):
            rows = ds(r * R, R)
            normed, _ = norm(xs_buf[s, rows, :].astype(F32))
            a1[s, rows, :] = (normed * prm[s, 2:3, :] + prm[s, 4:5, :]).astype(BF16)

        loop(4, body)
        normed, inv = norm(xs_buf[s, own, :].astype(F32))
        n1[s] = normed
        i1[s] = jnp.broadcast_to(inv, (R, 128))

    def attention(s):
        def body(h):
            b = 2 * h + s
            bias = jnp.concatenate(
                [prm[b, 7:8, 0:128], jnp.zeros((1, 128), F32), prm[b, 7:8, 128:256]], axis=1
            )
            qkv[s, h] = (dot_nn(a1[s], wq[b]) + bias).astype(BF16)
            query, key, value = qkv[s, h, :, 0:128], qkv[s, h, :, 128:256], qkv[s, h, :, 256:384]
            parts = []
            for e in (0, 1):
                scores = dot_nt(pick_head(query, e), key) * SCALE + mask[...]
                weights = jnp.exp(scores - jnp.max(scores, axis=-1, keepdims=True))
                probs = (weights / jnp.sum(weights, axis=-1, keepdims=True)).astype(BF16)
                prob[s, h, e] = probs
                parts.append(dot_nn(probs, value))
            mix[s, h] = jnp.where(low_lanes, parts[0], parts[1]).astype(BF16)

        loop(2, body)

    def partial(k, tile):
        def body(n):
            cols = ds(n * 256, 256)
            value = tile(cols)
            acc[:, cols] = value
            rs_out[k // 2, :, cols] = value.astype(BF16)

        loop(4, body)

    def feed_up(s):
        def body(i):
            h, n = lax.div(i, 2), lax.rem(i, 2)
            b = 2 * h + s
            cols = ds(n * 256, 256)
            u = dot_nn(a2[s], wu[b, :, cols]) + prm[b, 6:7, cols]
            th = jnp.tanh(GELU_COEF * (u + CUBIC_COEF * u * u * u))
            hid[s, h, :, cols] = (0.5 * u * (1.0 + th)).astype(BF16)
            slope[s, h, :, cols] = 0.5 * (1.0 + th) + 0.5 * u * (1.0 - th * th) * GELU_COEF * (
                1.0 + 3.0 * CUBIC_COEF * u * u
            )

        loop(4, body)

    def forward(s, hooks):
        w_forward(s, WQ)
        w_forward(s, WO)
        first_norm(s)
        w_ready(s, WQ)
        attention(s)
        w_ready(s, WO)
        partial(4 * s, lambda cols: dot_nn(mix[s, 0], wo[s, :, cols]) + dot_nn(mix[s, 1], wo[s + 2, :, cols]))
        k = 4 * s
        rs_start(k)
        hooks[0]()
        w_forward(s, WU)
        middle = xs_buf[s, own, :].astype(F32) + rs_finish(k) + prm[s, 0:1, :]
        yrow[...] = middle
        normed, inv = norm(middle)
        n2[s] = normed
        i2[s] = jnp.broadcast_to(inv, (R, 128))
        a2[s, own, :] = (normed * prm[s, 3:4, :] + prm[s, 5:6, :]).astype(BF16)
        ag_start(k + 1, a2.at[s])
        w_forward(s, WD)
        w_ready(s, WU)
        ag_finish(k + 1, a2.at[s])
        feed_up(s)
        w_ready(s, WD)
        partial(k + 2, lambda cols: dot_nn(hid[s, 0], wd[s, :, cols]) + dot_nn(hid[s, 1], wd[s + 2, :, cols]))
        rs_start(k + 2)
        result = (yrow[...] + rs_finish(k + 2) + prm[s, 1:2, :]).astype(BF16)
        target = xs_buf.at[1] if s == 0 else xo
        target[own, :] = result
        ag_start(k + 3, target)

    load_x.wait()
    for d in (1, 2, 3):
        send_prm(d).wait_recv()

    forward(0, [lambda: w_send_all(1)])
    ag_finish(3, xs_buf.at[1])
    out_start(0, 0, xs_buf.at[1], so_out)
    forward(1, [lambda: None])
    load_g.wait()

    def backward(s, k, hooks):
        def grad_up_tile(i):
            h, n = lax.div(i, 2), lax.rem(i, 2)
            b = 2 * h + s
            cols = ds(n * 256, 256)
            value = (dot_nt(g_buf[s], wd[b, cols, :]) * slope[s, h, :, cols]).astype(BF16)
            du[h, :, cols] = value

        loop(4, grad_up_tile)
        partial(k, lambda cols: dot_nt(du[0], wu[s, cols, :]) + dot_nt(du[1], wu[s + 2, cols, :]))
        rs_start(k)

        def grad_down(i):
            h, n = lax.div(i, 2), lax.rem(i, 2)
            rows = ds(n * 256, 256)
            gd[s, h, rows, :] = dot_tn(hid[s, h, :, rows], g_buf[s]).astype(BF16)

        loop(4, grad_down)
        gc_start(s, WD)

        def grad_up(i):
            h, n = lax.div(i, 4), lax.rem(i, 4)
            rows = ds(n * 256, 256)
            gu[s, h, rows, :] = dot_tn(a2[s, :, rows], du[h]).astype(BF16)

        loop(8, grad_up)
        gc_start(s, WU)
        for h in (0, 1):
            sm[s, 6:7, h * 512 : h * 512 + 512] = jnp.sum(du[h].astype(F32), axis=0, keepdims=True)
        hooks[0]()

        top = g_buf[s, own, :].astype(F32)
        sm[s, 1:2, :] = jnp.sum(top, axis=0, keepdims=True)
        g_second = rs_finish(k)
        normed = n2[s]
        sm[s, 3:4, :] = jnp.sum(g_second * normed, axis=0, keepdims=True)
        sm[s, 5:6, :] = jnp.sum(g_second, axis=0, keepdims=True)
        dy = top + norm_back(g_second, normed, i2[s, :, 0:1], prm[s, 3:4, :])
        dyrow[...] = dy
        sm[s, 0:1, :] = jnp.sum(dy, axis=0, keepdims=True)
        dyb[s, own, :] = dy.astype(BF16)
        ag_start(k + 1, dyb.at[s])
        hooks[1]()
        ag_finish(k + 1, dyb.at[s])

        def attention_back(h):
            b = 2 * h + s
            go[s, h] = dot_tn(mix[s, h], dyb[s]).astype(BF16)
            grad_mix = dot_nt(dyb[s], wo[b]).astype(BF16)
            query, key, value = qkv[s, h, :, 0:128], qkv[s, h, :, 128:256], qkv[s, h, :, 256:384]
            parts = []
            for e in (0, 1):
                probs = prob[s, h, e]
                wide = probs.astype(F32)
                grad_prob = dot_nt(pick_head(grad_mix, e), value)
                delta = jnp.sum(wide * grad_prob, axis=-1, keepdims=True)
                grad_scores = (wide * (grad_prob - delta) * SCALE).astype(BF16)
                parts.append((dot_nn(grad_scores, key), dot_tn(grad_scores, query), dot_tn(probs, grad_mix)))
            for j in range(3):
                both = jnp.where(low_lanes, parts[0][j], parts[1][j]).astype(BF16)
                dqkv[h, :, j * 128 : j * 128 + 128] = both

        loop(2, attention_back)
        partial(k + 2, lambda cols: dot_nt(dqkv[0], wq[s, cols, :]) + dot_nt(dqkv[1], wq[s + 2, cols, :]))
        rs_start(k + 2)
        gc_start(s, WO)

        def grad_qkv(i):
            h, n = lax.div(i, 4), lax.rem(i, 4)
            rows = ds(n * 256, 256)
            gq[s, h, rows, :] = dot_tn(a1[s, :, rows], dqkv[h]).astype(BF16)

        loop(8, grad_qkv)
        gc_start(s, WQ)
        for h in (0, 1):
            sums = jnp.sum(dqkv[h].astype(F32), axis=0, keepdims=True)
            sm[s, 7:8, h * 256 : h * 256 + 128] = sums[:, 0:128]
            sm[s, 7:8, h * 256 + 128 : h * 256 + 256] = sums[:, 256:384]
        hooks[2]()
        g_first = rs_finish(k + 2)
        normed = n1[s]
        sm[s, 2:3, :] = jnp.sum(g_first * normed, axis=0, keepdims=True)
        sm[s, 4:5, :] = jnp.sum(g_first, axis=0, keepdims=True)
        low = dyrow[...] + norm_back(g_first, normed, i1[s, :, 0:1], prm[s, 2:3, :])
        target = g_buf.at[0] if s == 1 else ig0
        target[own, :] = low.astype(BF16)
        ag_start(k + 3, target)
        hooks[3]()
        ag_finish(k + 3, target)

    def b1_0():
        ag_finish(7, xo)
        out_start(1, 1, xo, so_out)

    def b1_1():
        gy_start(1, WD)

    def b1_2():
        gy_start(1, WU)

    def b1_3():
        gy_start(1, WO)
        gy_start(1, WQ)

    backward(1, 8, [b1_0, b1_1, b1_2, b1_3])
    out_start(2, 1, g_buf.at[0], ig_out)

    def b0_0():
        gz_start(1, WD)

    def b0_1():
        gy_start(0, WD)
        gy_start(0, WU)
        gz_start(1, WU)

    def b0_2():
        gz_start(1, WO)
        gz_start(1, WQ)
        gy_start(0, WO)

    def b0_3():
        gy_start(0, WQ)
        for k in (WD, WU, WO, WQ):
            ga_start(1, k)
        gz_start(0, WD)

    backward(0, 12, [b0_0, b0_1, b0_2, b0_3])
    out_start(3, 0, ig0, ig_out)

    def small_copy(i, src, dst, device):
        return remote(src, dst, sm_s.at[i], sm_r.at[i], device)

    small_y = [small_copy(d - 1, sm, smy.at[d - 1], dev(x, yp(d), z, c)) for d in (1, 2, 3)]
    small_z = [
        small_copy(3 + j, sm2, smz.at[j], dev(x, y, zp(dz), lax.rem(c + dc, 2))) for j, (dz, dc) in enumerate(zc_peers)
    ]
    small_x = [small_copy(10 + d - 1, sm3, smx.at[d - 1], dev(xp(d), y, z, c)) for d in (1, 2, 3)]
    for copy in small_y:
        copy.start()
    gz_start(0, WU)
    for copy in small_y:
        copy.wait_recv()
    sm2[...] = sm[...] + smy[0] + smy[1] + smy[2]
    for copy in small_z:
        copy.start()
    gz_start(0, WO)
    gz_start(0, WQ)
    for copy in small_z:
        copy.wait_recv()
    total = sm2[...]
    for j in range(7):
        total = total + smz[j]
    sm3[...] = total
    for copy in small_x:
        copy.start()
    for k in (WD, WU, WO, WQ):
        ga_start(0, k)
    for copy in small_x:
        copy.wait_recv()
    shared = sm3[p] + smx[0, p] + smx[1, p] + smx[2, p]
    small_out[...] = shared
    up_out[...] = sm3[p, 6:7, ds(h_me * 512, 512)]
    qv_out[0:1, :] = sm3[p, 7:8, pl.ds(pl.multiple_of(h_me * 256, 128), 128)]
    qv_out[1:2, :] = sm3[p, 7:8, pl.ds(pl.multiple_of(h_me * 256 + 128, 128), 128)]

    for s in (0, 1):
        for k in range(4):
            ga_finish(s, k)
    out_finish(0, 0, xs_buf.at[1], so_out)
    out_finish(1, 1, xo, so_out)
    out_finish(2, 1, g_buf.at[0], ig_out)
    out_finish(3, 0, ig0, ig_out)
    for d in (1, 2, 3):
        send_prm(d).wait_send()
        for k in range(4):
            w_send(k, d).wait_send()
    for s in (0, 1):
        for k in range(4):
            @pl.when(p == s)
            def _():
                w_pass(k, 2).wait_send()
                for d in (1, 2, 3):
                    gz_copy(s, k, d).wait_send()
                for j in range(7):
                    ga_copy(s, k, j).wait_send()

            @pl.when(p != s)
            def _():
                for d in (1, 3):
                    w_pass(k, d).wait_send()

            for h in (0, 1):
                gc_copy(s, k, h).wait_send()

                @pl.when(y != 2 * h + s)
                def _():
                    gy_copy(s, k, h).wait_send()

    for k in range(0, 16, 2):
        for d in (1, 2, 3):
            rs_copy(k, d).wait_send()
    for k, ref in ((1, a2.at[0]), (3, xs_buf.at[1]), (5, a2.at[1]), (7, xo), (9, dyb.at[1]), (11, g_buf.at[0]),
                   (13, dyb.at[0]), (15, ig0)):
        for d in (1, 2, 3):
            ag_copy(k, ref, d).wait_send()
    for copy in small_y + small_z + small_x:
        copy.wait_send()


def run(x_in, seg, wq, qvb, wo, outb, wu, upb, wd, downb, gain, shift, og):
    any_spec = pl.BlockSpec(memory_space=pl.ANY)
    vmem = pl.BlockSpec(memory_space=pltpu.VMEM)
    V = pltpu.VMEM
    dma = pltpu.SemaphoreType.DMA
    tokens = x_in.shape[0]

    def kinds(lead, shrink):
        return [V(tuple(lead) + (ROWS[k] // shrink, COLS[k]), BF16) for k in range(4)]

    scratch = kinds((4,), 1)
    scratch += [
        V((4, 8, D), F32), V((SEQ, SEQ), F32),
        V((2, SEQ, D), BF16), V((2, SEQ, D), BF16), V((2, SEQ, D), BF16), V((2, SEQ, D), BF16), V((2, SEQ, D), BF16),
        V((SEQ, D), BF16), V((SEQ, D), BF16),
        V((2, 2, SEQ, 384), BF16), V((2, 2, 2, SEQ, SEQ), BF16), V((2, 2, SEQ, 128), BF16),
        V((2, 2, SEQ, 512), BF16), V((2, 2, SEQ, 512), F32),
        V((2, SEQ, 512), BF16), V((2, SEQ, 384), BF16), V((SEQ, D), F32),
        V((8, SEQ, D), BF16), V((8, 3, R, D), BF16),
        V((2, R, D), F32), V((2, R, D), F32), V((2, R, 128), F32), V((2, R, 128), F32), V((R, D), F32), V((R, D), F32),
    ]
    scratch += kinds((2, 2), 1) + kinds((2, 2), 2) + kinds((3,), 2) + kinds((3,), 8)
    scratch += [V((2, 8, D), F32)] * 3 + [V((3, 2, 8, D), F32), V((7, 2, 8, D), F32), V((3, 2, 8, D), F32)]
    scratch += [
        dma((48,)), dma((48,)), dma((12,)), dma((12,)), dma((12,)), dma((12,)), dma((3,)), dma((3,)), dma((6,)),
        dma((16,)), dma((16,)), dma((16,)), dma((12,)), dma((12,)), dma((12,)), dma((28,)), dma((28,)), dma((4,)),
        dma((13,)), dma((13,)), dma((12,)), dma((12,)), dma((4,)),
    ]
    return pl.pallas_call(
        kernel,
        out_shape=(
            jax.ShapeDtypeStruct((tokens, D), BF16),
            jax.ShapeDtypeStruct((tokens, D), BF16),
            *[jax.ShapeDtypeStruct((ROWS[k], COLS[k]), BF16) for k in range(4)],
            jax.ShapeDtypeStruct((8, D), F32),
            jax.ShapeDtypeStruct((1, 512), F32),
            jax.ShapeDtypeStruct((2, 128), F32),
        ),
        in_specs=[any_spec, vmem, any_spec, vmem, any_spec, vmem, any_spec, vmem, any_spec, vmem, vmem, vmem, any_spec],
        out_specs=(any_spec,) * 6 + (vmem,) * 3,
        scratch_shapes=scratch,
        compiler_params=pltpu.CompilerParams(collective_id=0, has_side_effects=True, vmem_limit_bytes=64 * 1024 * 1024),
    )(x_in, seg, wq, qvb, wo, outb, wu, upb, wd, downb, gain, shift, og)


def on_device(
    section_input, segment_ids, w_qkv, qv_bias, w_out, out_bias, w_up, up_bias, w_down, down_bias, norm_gains,
    norm_shifts, out_grad,
):
    so, ig, gq, go, gu, gd, small, up, qv = run(
        section_input, segment_ids.reshape(-1, SEQ), w_qkv.reshape(D, 384), qv_bias[0], w_out[0], out_bias, w_up[0],
        up_bias, w_down[0], down_bias, norm_gains[0], norm_shifts[0], out_grad,
    )
    return (
        so[None],
        ig[None],
        gq.astype(F32).reshape(1, D, 3, 128),
        qv[None],
        go.astype(F32)[None],
        small[0:1],
        gu.astype(F32)[None],
        up,
        gd.astype(F32)[None],
        small[1:2],
        small[None, 2:4],
        small[None, 4:6],
    )


def solution(mesh):
    placed = (
        P("dp", None),
        P("dp"),
        P("pipe", None, None, "tensor"),
        P("pipe", None, "tensor"),
        P("pipe", "tensor", None),
        P("pipe", None),
        P("pipe", None, "tensor"),
        P("pipe", "tensor"),
        P("pipe", "tensor", None),
        P("pipe", None),
        P("pipe", None, None),
        P("pipe", None, None),
        P("dp", None),
    )
    return jax.shard_map(
        on_device,
        mesh=mesh,
        in_specs=placed,
        out_specs=(
            P("pipe", "dp", None),
            P("pipe", "dp", None),
            P("pipe", None, None, "tensor"),
            P("pipe", None, "tensor"),
            P("pipe", "tensor", None),
            P("pipe", None),
            P("pipe", None, "tensor"),
            P("pipe", "tensor"),
            P("pipe", "tensor", None),
            P("pipe", None),
            P("pipe", None, None),
            P("pipe", None, None),
        ),
        check_vma=False,
    )
```

time: 1980 us -> 354 us (0.18)
  waiting for transfers between devices: 1640 us -> 0 us
  Pallas kernels: 0 us -> 332 us
  matrix products: 134 us -> 0 us
  other arithmetic: 103 us -> 4.97 us
  blocking collectives: 26.1 us -> 0 us
  local copies, waits for them, and re-layouts: 35.6 us -> 15.3 us
    psum x20 -> x0, waiting for transfers between devices: 1590 us -> none  [the longest x19 1560 us: combine(): lax.psum(partial_rows.astype(jnp.bfloat16), 'tensor').astype(jnp.float32)]
    pallas_call x0 -> x1, Pallas kernels: none -> 332 us  [run(): pl.pallas_call(kernel, out_shape=(jax.ShapeDtypeStruct((tokens, D), BF16)...]
    dot_general x85 -> x0, matrix products: 130 us -> none  [the longest x5 15.6 us: on_device(): jnp.einsum('tf,td->fd', hidden, cotangent, preferred_element_type=jnp.flo...]
    reduce_sum x48 -> x0, other arithmetic: 65.6 us -> none  [the longest x10 13.5 us: layer_norm(): centred = rows_in - jnp.mean(rows_in, axis=-1, keepdims=True)]
    ppermute x8 -> x0, waiting for transfers between devices: 44.3 us -> none  [passed_along(): return lax.ppermute(x, axis, pairs)]
    psum x1 -> x0, blocking collectives: 26.1 us -> none  [on_device(): lax.psum(g_qv.astype(jnp.bfloat16), 'dp').astype(jnp.float32)]
  transfers between devices with their start and end apart: 28 -> 0, of which waited for: 28 -> 0; matrix products, arithmetic and copies ran while one was open for 3% -> 0% of each run, Pallas kernels for 0% -> 0%
where the time goes in v1:
time: 354 us; the launch traced here: 353 us
  Pallas kernels  332 us (94%)
  local copies, waits for them, and re-layouts  15.3 us (4%)
  other arithmetic  4.97 us (1%)
    pallas_call x1, Pallas kernels, run(): pl.pallas_call(kernel, out_shape=(jax.ShapeDtypeStruct((tokens, D), BF16)...  332 us
    unnamed x18, local copies, waits for them, and re-layouts  8.62 us

profile of v1, /device:TPU:1, one launch (start us, length us, event | category | flops | bytes accessed | tf_op | source)
XLA Modules:
  0.0 353.1 jit_solution(1981942151131882571)
XLA Ops:
  0.6 1.3 reshape.36.seg_in
  1.9 1.4 copy.27
  3.3 1.2 copy.28.wq_in
  4.5 332.1 %shard_map.220 = (bf16[1024,1024]{1,0:T(8,128)(2,1)}, bf16[1024,1024]{1,0:T(8,128)(2,1)}, bf16[1024,384]{1,0:T(8,128)(2,1)}, bf16[128,1024]{1,0:T(8,128)(2,1)}, ...) custom-call(bf16[1024,1024]{1,0:T(8,128)(2,1)} %x_in.1, ...), custom_call_target="tpu_custom_call" | custom-call | tf_op jit(solution)/shard_map/pallas_call | solution.py:679
  336.6 1.4 fusion
  338.0 1.4 slice_bitcast_fusion
  339.5 1.8 bitcast_convert_fusion.2
  341.3 1.4 copy.29
  342.7 0.0 copy-start.3
  342.7 1.6 copy.30
  344.3 0.0 copy-done.3
  344.3 0.0 copy-start.2
  344.3 1.6 bitcast_convert_fusion.1
  345.9 0.0 copy-done.2
  345.9 0.0 copy-start.1
  345.9 1.6 bitcast_convert_fusion
  347.5 0.8 copy-done.1
  348.3 0.0 copy-start
  348.3 1.3 copy.35
  349.6 1.0 copy-done
  350.6 0.0 copy-start.5
  350.6 0.0 copy-start.4
  350.6 1.3 copy.36
  351.9 0.0 copy-done.5
  351.9 0.6 copy.37
  352.5 0.0 copy-done.4
  352.5 0.6 copy.38
Async XLA Ops:
  342.7 1.6 copy-start.3
  344.3 1.6 copy-start.2
  345.9 2.3 copy-start.1
  348.3 2.3 copy-start
  350.6 1.3 copy-start.5
  350.6 1.9 copy-start.4

commit v2 on v1

--- a/solution.py
+++ b/solution.py
@@ -60,8 +60,8 @@
     so_out, ig_out, gq_out, go_out, gu_out, gd_out, small_out, up_out, qv_out,
     wq, wo, wu, wd, prm, mask, xs_buf, g_buf, a1, a2, dyb, xo, ig0, qkv, prob, mix, hid, slope, du, dqkv, acc,
     rs_out, rs_in, n1, n2, i1, i2, yrow, dyrow,
-    gq, go, gu, gd, cq, co, cu, cd, yq, yo, yu, yd, zq, zo, zu, zd, sm, sm2, sm3, smy, smz, smx,
-    x_s, x_r, wy_s, wy_r, wc_s, wc_r, pr_s, pr_r, loc, gc_s, gc_r, gy_s, gy_r, gz_s, gz_r, ga_s, ga_r, gl,
+    gq, go, gu, gd, cq, co, cu, cd, yq, yo, yu, yd, zq, zo, zu, zd, fq, fo, fu, fd, sm, sm2, sm3, smy, smz, smx,
+    x_s, x_r, wy_s, wy_r, wz_s, wz_r, wc_s, wc_r, pr_s, pr_r, loc, gc_s, gc_r, gy_s, gy_r, gz_s, gz_r, ga_s, ga_r, gf_s, gf_r, gl,
     sm_s, sm_r, o_s, o_r, o_l,
 ):
     p = lax.axis_index("pipe")
@@ -97,6 +97,7 @@
     c_all = (cq, co, cu, cd)
     y_all = (yq, yo, yu, yd)
     z_all = (zq, zo, zu, zd)
+    fin = (fq, fo, fu, fd)
     g_outs = (gq_out, go_out, gu_out, gd_out)
 
     zc_peers = [(dz, dc) for dz in range(4) for dc in range(2) if (dz, dc) != (0, 0)]
@@ -137,14 +138,28 @@
     def half_rows(k, which):
         return ds(which * (ROWS[k] // 2), ROWS[k] // 2)
 
+    even = lax.rem(z, 2)
+
+    def quarter_rows(k, which):
+        return ds(c * (ROWS[k] // 2) + which * (ROWS[k] // 4), ROWS[k] // 4)
+
+    def eighth_rows(k, which, j):
+        q = ROWS[k] // 8
+        return ds(c * (ROWS[k] // 2) + which * (2 * q) + j * q, q)
+
     def w_send(k, d):
-        rows = half_rows(k, c)
+        rows = quarter_rows(k, even)
         i = k * 3 + d - 1
         return remote(w_in[k].at[rows], w_all[k].at[y, rows], wy_s.at[i], wy_r.at[i], dev(x, yp(d), z, c))
 
-    def w_pass(k, d):
-        rows = half_rows(k, c)
-        i = k * 3 + d - 1
+    def w_side(k, d, j):
+        i = (k * 3 + d - 1) * 2 + j
+        block = w_all[k].at[lax.rem(y - d + 4, 4), eighth_rows(k, even, j)]
+        return remote(block, block, wz_s.at[i], wz_r.at[i], dev(x, y, zp(1 if j == 0 else 3), c))
+
+    def w_pass(k, d, j):
+        i = (k * 3 + d - 1) * 3 + j
+        rows = quarter_rows(k, even) if j == 0 else eighth_rows(k, 1 - even, j - 1)
         block = w_all[k].at[lax.rem(y - d + 4, 4), rows]
         return remote(block, block, wc_s.at[i], wc_r.at[i], core_peer)
 
@@ -155,28 +170,43 @@
                 for d in (2, 1, 3):
                     w_send(k, d).start()
 
-    def w_forward(s, k):
+    def w_each(s, act):
         @pl.when(p == s)
         def _():
-            w_send(k, 2).wait_recv()
-            w_pass(k, 2).start()
+            act(2)
 
         @pl.when(p != s)
         def _():
-            for d in (1, 3):
-                w_send(k, d).wait_recv()
-                w_pass(k, d).start()
+            act(1)
+            act(3)
+
+    def w_spread(s, k):
+        def act(d):
+            w_send(k, d).wait_recv()
+            for j in (0, 1):
+                w_side(k, d, j).start()
+            w_pass(k, d, 0).start()
+
+        w_each(s, act)
+
+    def w_hand_over(s, k):
+        def act(d):
+            for j in (0, 1):
+                w_side(k, d, j).wait_recv()
+                w_pass(k, d, 1 + j).start()
+
+        w_each(s, act)
 
     def w_ready(s, k):
         @pl.when(p == s)
         def _():
             load_w[k].wait()
-            w_pass(k, 2).wait_recv()
-
-        @pl.when(p != s)
-        def _():
-            for d in (1, 3):
-                w_pass(k, d).wait_recv()
+
+        def act(d):
+            for j in (0, 1, 2):
+                w_pass(k, d, j).wait_recv()
+
+        w_each(s, act)
 
     def rs_copy(k, d):
         dest = xp(d)
@@ -298,18 +328,18 @@
             for d in (2, 1, 3):
                 gz_copy(s, k, d).start()
 
-    def ga_copy(s, k, j):
-        dz, dc = zc_peers[j]
-        i = k * 7 + j
-        rows = piece(k, z)
-        return remote(
-            g_all[k].at[s, h_me, rows], g_outs[k].at[rows], ga_s.at[i], ga_r.at[i],
-            dev(x, y, zp(dz), lax.rem(c + dc, 2)),
-        )
-
-    def ga_local(s, k):
-        rows = piece(k, z)
-        return pltpu.make_async_copy(g_all[k].at[s, h_me, rows], g_outs[k].at[rows], gl.at[k])
+    def ga_copy(k, d):
+        i = k * 3 + d - 1
+        block = fin[k].at[piece(k, z)]
+        return remote(block, block, ga_s.at[i], ga_r.at[i], dev(x, y, zp(d), c))
+
+    def gf_copy(k):
+        rows = half_rows(k, c)
+        return remote(fin[k].at[rows], g_outs[k].at[rows], gf_s.at[k], gf_r.at[k], core_peer)
+
+    def gf_local(k):
+        rows = half_rows(k, c)
+        return pltpu.make_async_copy(fin[k].at[rows], g_outs[k].at[rows], gl.at[k])
 
     def ga_start(s, k):
         @pl.when(p == s)
@@ -317,19 +347,27 @@
             q = ROWS[k] // 8
             for d in (1, 3, 2):
                 gz_copy(s, k, d).wait_recv()
-            sum_rows(
-                k, g_all[k].at[s, h_me], c * (ROWS[k] // 2) + z * q, [z_all[k].at[j] for j in range(3)], q
-            )
-            for j in range(7):
-                ga_copy(s, k, j).start()
-            ga_local(s, k).start()
-
-    def ga_finish(s, k):
+            rows = piece(k, z)
+            total = g_all[k][s, h_me, rows, :].astype(F32)
+            for j in range(3):
+                total = total + z_all[k][j].astype(F32)
+            fin[k][rows, :] = total.astype(BF16)
+            for d in (2, 1, 3):
+                ga_copy(k, d).start()
+
+    def gf_start(s, k):
         @pl.when(p == s)
         def _():
-            ga_local(s, k).wait()
-            for j in range(7):
-                ga_copy(s, k, j).wait_recv()
+            for d in (1, 3, 2):
+                ga_copy(k, d).wait_recv()
+            gf_copy(k).start()
+            gf_local(k).start()
+
+    def gf_finish(k):
+        gf_local(k).wait()
+        gf_copy(k).wait()
+        for d in (1, 2, 3):
+            ga_copy(k, d).wait_send()
 
     w_send_all(0)
 
@@ -399,17 +437,16 @@
         loop(4, body)
 
     def forward(s, hooks):
-        w_forward(s, WQ)
-        w_forward(s, WO)
+        hooks[0]()
         first_norm(s)
         w_ready(s, WQ)
         attention(s)
+        hooks[4]()
         w_ready(s, WO)
         partial(4 * s, lambda cols: dot_nn(mix[s, 0], wo[s, :, cols]) + dot_nn(mix[s, 1], wo[s + 2, :, cols]))
         k = 4 * s
         rs_start(k)
-        hooks[0]()
-        w_forward(s, WU)
+        hooks[1]()
         middle = xs_buf[s, own, :].astype(F32) + rs_finish(k) + prm[s, 0:1, :]
         yrow[...] = middle
         normed, inv = norm(middle)
@@ -417,13 +454,15 @@
         i2[s] = jnp.broadcast_to(inv, (R, 128))
         a2[s, own, :] = (normed * prm[s, 3:4, :] + prm[s, 5:6, :]).astype(BF16)
         ag_start(k + 1, a2.at[s])
-        w_forward(s, WD)
+        hooks[2]()
         w_ready(s, WU)
         ag_finish(k + 1, a2.at[s])
         feed_up(s)
+        hooks[5]()
         w_ready(s, WD)
         partial(k + 2, lambda cols: dot_nn(hid[s, 0], wd[s, :, cols]) + dot_nn(hid[s, 1], wd[s + 2, :, cols]))
         rs_start(k + 2)
+        hooks[3]()
         result = (yrow[...] + rs_finish(k + 2) + prm[s, 1:2, :]).astype(BF16)
         target = xs_buf.at[1] if s == 0 else xo
         target[own, :] = result
@@ -433,10 +472,43 @@
     for d in (1, 2, 3):
         send_prm(d).wait_recv()
 
-    forward(0, [lambda: w_send_all(1)])
+    def f0_0():
+        w_spread(0, WQ)
+        w_spread(0, WO)
+        w_hand_over(0, WQ)
+
+    def f0_1():
+        w_send_all(1)
+        w_spread(0, WU)
+
+    def f0_2():
+        w_hand_over(0, WU)
+        w_spread(0, WD)
+
+    def f0_2b():
+        w_hand_over(0, WO)
+
+    def f0_3():
+        w_spread(1, WQ)
+        w_spread(1, WO)
+
+    def f1_0():
+        pass
+
+    def f1_1():
+        w_hand_over(1, WU)
+        w_spread(1, WD)
+
+    def f1_2():
+        w_hand_over(1, WD)
+
+    forward(0, [f0_0, f0_1, f0_2, f0_3, f0_2b, lambda: w_hand_over(0, WD)])
+    w_hand_over(1, WQ)
+    w_hand_over(1, WO)
+    w_spread(1, WU)
     ag_finish(3, xs_buf.at[1])
     out_start(0, 0, xs_buf.at[1], so_out)
-    forward(1, [lambda: None])
+    forward(1, [f1_0, f1_1, f1_2, f1_0, f1_0, f1_0])
     load_g.wait()
 
     def backward(s, k, hooks):
@@ -564,6 +636,7 @@
         for k in (WD, WU, WO, WQ):
             ga_start(1, k)
         gz_start(0, WD)
+        gz_start(0, WU)
 
     backward(0, 12, [b0_0, b0_1, b0_2, b0_3])
     out_start(3, 0, ig0, ig_out)
@@ -578,7 +651,8 @@
     small_x = [small_copy(10 + d - 1, sm3, smx.at[d - 1], dev(xp(d), y, z, c)) for d in (1, 2, 3)]
     for copy in small_y:
         copy.start()
-    gz_start(0, WU)
+    for k in (WD, WU, WO, WQ):
+        gf_start(1, k)
     for copy in small_y:
         copy.wait_recv()
     sm2[...] = sm[...] + smy[0] + smy[1] + smy[2]
@@ -604,9 +678,10 @@
     qv_out[0:1, :] = sm3[p, 7:8, pl.ds(pl.multiple_of(h_me * 256, 128), 128)]
     qv_out[1:2, :] = sm3[p, 7:8, pl.ds(pl.multiple_of(h_me * 256 + 128, 128), 128)]
 
-    for s in (0, 1):
-        for k in range(4):
-            ga_finish(s, k)
+    for k in (WD, WU, WO, WQ):
+        gf_start(0, k)
+    for k in range(4):
+        gf_finish(k)
     out_finish(0, 0, xs_buf.at[1], so_out)
     out_finish(1, 1, xo, so_out)
     out_finish(2, 1, g_buf.at[0], ig_out)
@@ -619,16 +694,16 @@
         for k in range(4):
             @pl.when(p == s)
             def _():
-                w_pass(k, 2).wait_send()
                 for d in (1, 2, 3):
                     gz_copy(s, k, d).wait_send()
-                for j in range(7):
-                    ga_copy(s, k, j).wait_send()
-
-            @pl.when(p != s)
-            def _():
-                for d in (1, 3):
-                    w_pass(k, d).wait_send()
+
+            def sent(d):
+                for j in (0, 1):
+                    w_side(k, d, j).wait_send()
+                for j in (0, 1, 2):
+                    w_pass(k, d, j).wait_send()
+
+            w_each(s, sent)
 
             for h in (0, 1):
                 gc_copy(s, k, h).wait_send()
@@ -669,11 +744,11 @@
         V((8, SEQ, D), BF16), V((8, 3, R, D), BF16),
         V((2, R, D), F32), V((2, R, D), F32), V((2, R, 128), F32), V((2, R, 128), F32), V((R, D), F32), V((R, D), F32),
     ]
-    scratch += kinds((2, 2), 1) + kinds((2, 2), 2) + kinds((3,), 2) + kinds((3,), 8)
+    scratch += kinds((2, 2), 1) + kinds((2, 2), 2) + kinds((3,), 2) + kinds((3,), 8) + kinds((), 1)
     scratch += [V((2, 8, D), F32)] * 3 + [V((3, 2, 8, D), F32), V((7, 2, 8, D), F32), V((3, 2, 8, D), F32)]
     scratch += [
-        dma((48,)), dma((48,)), dma((12,)), dma((12,)), dma((12,)), dma((12,)), dma((3,)), dma((3,)), dma((6,)),
-        dma((16,)), dma((16,)), dma((16,)), dma((12,)), dma((12,)), dma((12,)), dma((28,)), dma((28,)), dma((4,)),
+        dma((48,)), dma((48,)), dma((12,)), dma((12,)), dma((24,)), dma((24,)), dma((36,)), dma((36,)), dma((3,)), dma((3,)), dma((6,)),
+        dma((16,)), dma((16,)), dma((16,)), dma((12,)), dma((12,)), dma((12,)), dma((12,)), dma((12,)), dma((4,)), dma((4,)), dma((4,)),
         dma((13,)), dma((13,)), dma((12,)), dma((12,)), dma((4,)),
     ]
     return pl.pallas_call(

time: 354 us -> 314 us (0.89)
  Pallas kernels: 332 us -> 293 us
    pallas_call x1, Pallas kernels: 332 us -> 293 us  [run(): pl.pallas_call(kernel, out_shape=(jax.ShapeDtypeStruct((tokens, D), BF16)...]
where the time goes in v2:
time: 314 us
  Pallas kernels  293 us (93%)
  local copies, waits for them, and re-layouts  15.3 us (5%)
  other arithmetic  4.97 us (2%)
    pallas_call x1, Pallas kernels, run(): pl.pallas_call(kernel, out_shape=(jax.ShapeDtypeStruct((tokens, D), BF16)...  293 us
    unnamed x18, local copies, waits for them, and re-layouts  8.62 us

profile of v2, /device:TPU:1, one launch (start us, length us, event | category | flops | bytes accessed | tf_op | source)
XLA Modules:
  0.0 313.6 jit_solution(1754202235692397537)
XLA Ops:
  0.6 1.3 reshape.36.seg_in
  1.9 1.4 copy.27
  3.3 1.2 copy.28.wq_in
  4.5 292.6 %shard_map.220 = (bf16[1024,1024]{1,0:T(8,128)(2,1)}, bf16[1024,1024]{1,0:T(8,128)(2,1)}, bf16[1024,384]{1,0:T(8,128)(2,1)}, bf16[128,1024]{1,0:T(8,128)(2,1)}, ...) custom-call(bf16[1024,1024]{1,0:T(8,128)(2,1)} %x_in.1, ...), custom_call_target="tpu_custom_call" | custom-call | tf_op jit(solution)/shard_map/pallas_call | solution.py:754
  297.1 1.4 fusion
  298.5 1.4 slice_bitcast_fusion
  299.9 1.8 bitcast_convert_fusion.2
  301.7 1.4 copy.29
  303.1 0.0 copy-start.3
  303.2 1.6 copy.30
  304.8 0.0 copy-done.3
  304.8 0.0 copy-start.2
  304.8 1.6 bitcast_convert_fusion.1
  306.4 0.0 copy-done.2
  306.4 0.0 copy-start.1
  306.4 1.6 bitcast_convert_fusion
  308.0 0.8 copy-done.1
  308.7 0.0 copy-start
  308.7 1.3 copy.35
  310.1 1.0 copy-done
  311.1 0.0 copy-start.5
  311.1 0.0 copy-start.4
  311.1 1.3 copy.36
  312.4 0.0 copy-done.5
  312.4 0.6 copy.37
  313.0 0.0 copy-done.4
  313.0 0.6 copy.38
Async XLA Ops:
  303.1 1.6 copy-start.3
  304.8 1.6 copy-start.2
  306.4 2.3 copy-start.1
  308.7 2.3 copy-start
  311.1 1.3 copy-start.5
  311.1 1.9 copy-start.4

commit v3 on v2

v3 whole, which is shorter than its diff:
```python
import jax
import jax.numpy as jnp
from jax import lax
from jax.experimental import pallas as pl
from jax.experimental.pallas import tpu as pltpu
from jax.sharding import PartitionSpec as P

MESH = pl.DeviceIdType.MESH
F32 = jnp.float32
BF16 = jnp.bfloat16

SEQ = 256
D = 1024
HALF = 128
R = 32
NORM_EPS = 1e-05
GELU_COEF = 0.7978845608028654
CUBIC_COEF = 0.044715
MASKED_SCORE = -1e30
SCALE = 0.125
WQ, WO, WU, WD = range(4)
ROWS = (1024, 128, 1024, 512)
COLS = (128, 1024, 512, 1024)
Z_FIRST = (WQ, WU)


def dot_nn(a, b):
    return jnp.dot(a, b, preferred_element_type=F32)


def dot_nt(a, b):
    return lax.dot_general(a, b, (((1,), (1,)), ((), ())), preferred_element_type=F32)


def dot_tn(a, b):
    return lax.dot_general(a, b, (((0,), (0,)), ((), ())), preferred_element_type=F32)


def loop(n, body):
    lax.fori_loop(0, n, lambda i, c: (body(i), c)[1], 0)


def ds(start, size):
    return pl.ds(pl.multiple_of(start, size), size)


def norm(rows):
    centred = rows - jnp.mean(rows, axis=-1, keepdims=True)
    inv = lax.rsqrt(jnp.mean(centred * centred, axis=-1, keepdims=True) + NORM_EPS)
    return centred * inv, inv


def norm_back(grad, normed, inv, gain):
    e = grad * gain
    return inv * (
        e - jnp.mean(e, axis=-1, keepdims=True) - normed * jnp.mean(e * normed, axis=-1, keepdims=True)
    )


def shape_of(k, rows):
    return (3, rows, 128) if k == WQ else (rows, COLS[k])


def at(k, rows):
    return (slice(None), rows) if k == WQ else (rows,)


def kernel(
    x_in, seg_in, wq_in, qvb_in, wo_in, outb_in, wu_in, upb_in, wd_in, downb_in, gain_in, shift_in, og_in,
    so_out, ig_out, gq_out, go_out, gu_out, gd_out, small_out,
    wq, wo, wu, wd, prm, mask, xs_buf, g_buf, a1, a2, dyb, xo, ig0, qkv, prob, mix, hid, slope, du, dqkv, dkv, acc,
    rs_out, rs_in, n1, n2, i1, i2, yrow, dyrow,
    gq, go, gu, gd, cq, co, cu, cd, yq, yo, yu, yd, zq, zo, zu, zd, fq, fo, fu, fd,
    sm, sm1, sm2, sm3, smc, smz, smy, smx,
    x_s, x_r, wy_s, wy_r, wz_s, wz_r, wc_s, wc_r, pr_s, pr_r, loc, gc_s, gc_r, gy_s, gy_r, gz_s, gz_r, ga_s, ga_r,
    gf_s, gf_r, gl, sm_s, sm_r, o_s, o_r, o_l, d_s, d_r, d_l,
):
    p = lax.axis_index("pipe")
    t = lax.axis_index("tensor")
    dp = lax.axis_index("dp")
    h_me, x = lax.div(t, 4), lax.rem(t, 4)
    z, c = lax.div(dp, 2), lax.rem(dp, 2)
    y = h_me * 2 + p

    def dev(xx, yy, zz, cc):
        return {"pipe": lax.rem(yy, 2), "tensor": lax.div(yy, 2) * 4 + xx, "dp": zz * 2 + cc}

    def xp(d):
        return lax.rem(x + d, 4)

    def yp(d):
        return lax.rem(y + d, 4)

    def zp(d):
        return lax.rem(z + d, 4)

    core_peer = dev(x, y, z, 1 - c)

    def remote(src, dst, ss, rs, device):
        return pltpu.make_async_remote_copy(
            src_ref=src, dst_ref=dst, send_sem=ss, recv_sem=rs, device_id=device, device_id_type=MESH
        )

    def stream(u):
        return pl.ds(u * HALF, HALF)

    def own(u):
        return ds(u * HALF + x * R, R)

    w_in = (wq_in, wo_in, wu_in, wd_in)
    w_all = (wq, wo, wu, wd)
    g_all = (gq, go, gu, gd)
    c_all = (cq, co, cu, cd)
    y_all = (yq, yo, yu, yd)
    z_all = (zq, zo, zu, zd)
    fin = (fq, fo, fu, fd)
    g_outs = (gq_out, go_out, gu_out, gd_out)
    grid_peers = [(dx, dy) for dx in range(4) for dy in range(4) if (dx, dy) != (0, 0)]

    barrier = pltpu.get_barrier_semaphore()
    peers = [dev(xp(dx), yp(dy), z, c) for dx, dy in grid_peers]
    peers += [dev(x, y, zp(d), c) for d in (1, 2, 3)] + [core_peer]
    for peer in peers:
        pl.semaphore_signal(barrier, inc=1, device_id=peer, device_id_type=MESH)

    load_x = pltpu.make_async_copy(x_in.at[ds(y * SEQ, SEQ)], xs_buf.at[0], loc.at[0])
    load_g = pltpu.make_async_copy(og_in.at[ds(y * SEQ, SEQ)], g_buf.at[1], loc.at[1])
    load_x.start()
    load_w = [pltpu.make_async_copy(w_in[k], w_all[k].at[y], loc.at[2 + k]) for k in range(4)]
    for copy in load_w:
        copy.start()
    load_g.start()

    prm[y] = jnp.zeros((8, D), F32)
    prm[y, 0:1, :] = outb_in[...]
    prm[y, 1:2, :] = downb_in[...]
    prm[y, 2:4, :] = gain_in[...]
    prm[y, 4:6, :] = shift_in[...]
    prm[y, 6:7, 0:512] = upb_in[...]
    prm[y, 7:8, 0:128] = qvb_in[0:1, :]
    prm[y, 7:8, 128:256] = qvb_in[1:2, :]
    sm[...] = jnp.zeros_like(sm)

    pl.semaphore_wait(barrier, len(peers))

    def send_prm(d):
        return remote(prm.at[y], prm.at[y], pr_s.at[d - 1], pr_r.at[d - 1], dev(x, yp(d), z, c))

    even = lax.rem(z, 2)

    def half_rows(k, which):
        return ds(which * (ROWS[k] // 2), ROWS[k] // 2)

    def quarter_rows(k, which):
        q = ROWS[k] // 4
        return pl.ds(pl.multiple_of(c * (2 * q) + which * q, q), q)

    def eighth_rows(k, which, j):
        q = ROWS[k] // 8
        return pl.ds(pl.multiple_of(c * (4 * q) + which * (2 * q) + j * q, q), q)

    def w_send(k, d):
        rows = at(k, quarter_rows(k, even))
        i = k * 3 + d - 1
        return remote(
            w_in[k].at[rows], w_all[k].at[(y,) + rows], wy_s.at[i], wy_r.at[i], dev(x, yp(d), z, c)
        )

    def w_block(k, d, rows):
        return w_all[k].at[(lax.rem(y - d + 4, 4),) + at(k, rows)]

    def w_side(k, d, j):
        i = (k * 3 + d - 1) * 2 + j
        block = w_block(k, d, eighth_rows(k, even, j))
        return remote(block, block, wz_s.at[i], wz_r.at[i], dev(x, y, zp(1 if j == 0 else 3), c))

    def w_pass(k, d, j):
        i = (k * 3 + d - 1) * 3 + j
        block = w_block(k, d, quarter_rows(k, even) if j == 0 else eighth_rows(k, 1 - even, j - 1))
        return remote(block, block, wc_s.at[i], wc_r.at[i], core_peer)

    def w_send_all(s):
        @pl.when(p == s)
        def _():
            for k in range(4):
                for d in (2, 1, 3):
                    w_send(k, d).start()

    def w_each(s, act):
        @pl.when(p == s)
        def _():
            act(2)

        @pl.when(p != s)
        def _():
            act(1)
            act(3)

    def w_spread(s, k):
        def act(d):
            w_send(k, d).wait_recv()
            for j in (0, 1):
                w_side(k, d, j).start()
            w_pass(k, d, 0).start()

        w_each(s, act)

    def w_hand_over(s, k):
        def act(d):
            for j in (0, 1):
                w_side(k, d, j).wait_recv()
                w_pass(k, d, 1 + j).start()

        w_each(s, act)

    def w_ready(s, k):
        @pl.when(p == s)
        def _():
            load_w[k].wait()

        def act(d):
            for j in (0, 1, 2):
                w_pass(k, d, j).wait_recv()

        w_each(s, act)

    def x_sem(k, u, d):
        return (k * 2 + u) * 3 + d - 1

    def rs_copy(k, u, d):
        dest = xp(d)
        i = x_sem(k, u, d)
        return remote(
            rs_out.at[k // 2, ds(u * HALF + dest * R, R)], rs_in.at[k // 2, u, d - 1], x_s.at[i], x_r.at[i],
            dev(dest, y, z, c),
        )

    def rs_start(k, u):
        for d in (2, 1, 3):
            rs_copy(k, u, d).start()

    def rs_finish(k, u):
        total = acc[own(u), :]
        for d in (1, 3, 2):
            rs_copy(k, u, d).wait_recv()
            total = total + rs_in[k // 2, u, d - 1].astype(F32)
        return total

    def ag_copy(k, u, ref, d):
        i = x_sem(k, u, d)
        block = ref.at[own(u)]
        return remote(block, block, x_s.at[i], x_r.at[i], dev(xp(d), y, z, c))

    def ag_start(k, u, ref):
        for d in (2, 1, 3):
            ag_copy(k, u, ref, d).start()

    def ag_finish(k, u, ref):
        for d in (1, 3, 2):
            ag_copy(k, u, ref, d).wait_recv()

    def out_copy(i, ref, out, d):
        j = i * 3 + d - 1
        return remote(ref, out.at[ds(y * SEQ, SEQ)], o_s.at[j], o_r.at[j], dev(x, yp(d), z, c))

    def out_local(i, ref, out):
        return pltpu.make_async_copy(ref, out.at[ds(y * SEQ, SEQ)], o_l.at[i])

    def out_start(i, s, ref, out):
        for d in (1, 2, 3):
            @pl.when(lax.rem(y + d, 2) == s)
            def _():
                out_copy(i, ref, out, d).start()

        @pl.when(p == s)
        def _():
            out_local(i, ref, out).start()

    def out_finish(i, s, ref, out):
        for d in (1, 2, 3):
            @pl.when(lax.rem(y + d, 2) == s)
            def _():
                out_copy(i, ref, out, d).wait_send()

        @pl.when(p == s)
        def _():
            out_local(i, ref, out).wait()
            for d in (1, 2, 3):
                out_copy(i, ref, out, d).wait_recv()

    def low_rows(u):
        return ds(y * SEQ + u * HALF + x * R, R)

    def low_copy(u, j):
        dx, dy = grid_peers[j]
        i = u * 15 + j
        return remote(ig0.at[own(u)], ig_out.at[low_rows(u)], d_s.at[i], d_r.at[i], dev(xp(dx), yp(dy), z, c))

    def low_local(u):
        return pltpu.make_async_copy(ig0.at[own(u)], ig_out.at[low_rows(u)], d_l.at[u])

    def low_start(u):
        for j, (dx, dy) in enumerate(grid_peers):
            @pl.when(lax.rem(y + dy, 2) == 0)
            def _():
                low_copy(u, j).start()

        @pl.when(p == 0)
        def _():
            low_local(u).start()

    def low_finish(u):
        for j, (dx, dy) in enumerate(grid_peers):
            @pl.when(lax.rem(y + dy, 2) == 0)
            def _():
                low_copy(u, j).wait_send()

        @pl.when(p == 0)
        def _():
            low_local(u).wait()
            for j in range(15):
                low_copy(u, j).wait_recv()

    def gc_copy(s, k, h):
        i = (s * 4 + k) * 2 + h
        return remote(
            g_all[k].at[(s, h) + at(k, half_rows(k, 1 - c))], c_all[k].at[s, h], gc_s.at[i], gc_r.at[i], core_peer
        )

    def gc_start(s, k):
        for h in (0, 1):
            gc_copy(s, k, h).start()

    def sum_rows(k, target, base, sources, rows, result=None):
        step = min(rows, 64)
        result = target if result is None else result

        def body(r):
            here = at(k, pl.ds(pl.multiple_of(base + r * step, 16), step))
            there = at(k, pl.ds(pl.multiple_of(r * step, 16), step))
            total = target[here].astype(F32)
            for source in sources:
                total = total + source[there].astype(F32)
            result[here] = total.astype(BF16)

        loop(rows // step, body)

    def piece_base(k, zz):
        return c * (ROWS[k] // 2) + zz * (ROWS[k] // 8)

    def piece(k, zz):
        return at(k, pl.ds(pl.multiple_of(piece_base(k, zz), 16), ROWS[k] // 8))

    def gy_copy(s, k, h):
        d = lax.rem(2 * h + s - y + 4, 4)
        i = (s * 4 + k) * 2 + h
        rows = piece(k, z) if k in Z_FIRST else at(k, half_rows(k, c))
        return remote(
            g_all[k].at[(s, h) + rows], y_all[k].at[d - 1], gy_s.at[i], gy_r.at[k * 3 + d - 1],
            dev(x, 2 * h + s, z, c),
        )

    def gy_arrived(k):
        for d in (1, 3, 2):
            slot = y_all[k].at[d - 1]
            remote(slot, slot, gy_s.at[0], gy_r.at[k * 3 + d - 1], dev(x, yp(d), z, c)).wait_recv()

    def gy_start(s, k, h):
        @pl.when(y != 2 * h + s)
        def _():
            gy_copy(s, k, h).start()

    def gz_copy(s, k, h, d):
        zz = zp(d)
        i = ((s * 4 + k) * 2 + h) * 3 + d - 1 if k in Z_FIRST else 48 + k * 3 + d - 1
        block = h if k in Z_FIRST else h_me
        slot = z_all[k].at[s, h, d - 1] if k in Z_FIRST else z_all[k].at[d - 1]
        return remote(g_all[k].at[(s, block) + piece(k, zz)], slot, gz_s.at[i], gz_r.at[i], dev(x, y, zz, c))

    def ga_copy(k, d):
        i = k * 3 + d - 1
        block = fin[k].at[piece(k, z)]
        return remote(block, block, ga_s.at[i], ga_r.at[i], dev(x, y, zp(d), c))

    def gf_copy(k):
        rows = at(k, half_rows(k, c))
        return remote(fin[k].at[rows], g_outs[k].at[rows], gf_s.at[k], gf_r.at[k], core_peer)

    def gf_local(k):
        rows = at(k, half_rows(k, c))
        return pltpu.make_async_copy(fin[k].at[rows], g_outs[k].at[rows], gl.at[k])

    def stage1(s, k):
        for h in (0, 1):
            gc_copy(s, k, h).wait_recv()
            sum_rows(k, g_all[k].at[s, h], c * (ROWS[k] // 2), [c_all[k].at[s, h]], ROWS[k] // 2)
            if k in Z_FIRST:
                for d in (2, 1, 3):
                    gz_copy(s, k, h, d).start()
            else:
                gy_start(s, k, h)

    def stage2(s, k):
        q = ROWS[k] // 8
        if k in Z_FIRST:
            for h in (0, 1):
                for d in (1, 3, 2):
                    gz_copy(s, k, h, d).wait_recv()
                sum_rows(k, g_all[k].at[s, h], piece_base(k, z), [z_all[k].at[s, h, j] for j in range(3)], q)
                gy_start(s, k, h)
        else:
            @pl.when(p == s)
            def _():
                gy_arrived(k)
                sum_rows(
                    k, g_all[k].at[s, h_me], c * (4 * q), [y_all[k].at[j] for j in range(3)], 4 * q
                )
                for d in (2, 1, 3):
                    gz_copy(s, k, 0, d).start()

    def stage3(s, k):
        @pl.when(p == s)
        def _():
            if k in Z_FIRST:
                gy_arrived(k)
                slots = [y_all[k].at[j] for j in range(3)]
            else:
                for d in (1, 3, 2):
                    gz_copy(s, k, 0, d).wait_recv()
                slots = [z_all[k].at[j] for j in range(3)]
            sum_rows(k, g_all[k].at[s, h_me], piece_base(k, z), slots, ROWS[k] // 8, fin[k])
            for d in (2, 1, 3):
                ga_copy(k, d).start()

    def stage4(s, k):
        @pl.when(p == s)
        def _():
            for d in (1, 3, 2):
                ga_copy(k, d).wait_recv()
            gf_copy(k).start()
            gf_local(k).start()

    def gf_finish(k):
        gf_local(k).wait()
        gf_copy(k).wait()
        for d in (1, 2, 3):
            ga_copy(k, d).wait_send()

    w_send_all(0)
    for d in (1, 2, 3):
        send_prm(d).start()

    seg = jnp.concatenate([seg_in[pl.ds(2 * y, 1), :], seg_in[pl.ds(2 * y + 1, 1), :]], axis=1).astype(F32)
    seg_b = jnp.broadcast_to(seg, (SEQ, SEQ))
    rows_i = lax.broadcasted_iota(jnp.int32, (SEQ, SEQ), 0)
    cols_i = lax.broadcasted_iota(jnp.int32, (SEQ, SEQ), 1)
    mask[...] = jnp.where((rows_i >= cols_i) & (seg_b == seg_b.T), 0.0, MASKED_SCORE)

    def low_lanes(rows):
        return lax.broadcasted_iota(jnp.int32, (rows, 128), 1) < 64

    def pick_head(value, e):
        keep = low_lanes(value.shape[0])
        keep = keep if e == 0 else jnp.logical_not(keep)
        return jnp.where(keep, value, jnp.zeros_like(value))

    def planes(b, rows):
        return jnp.concatenate([wq[b, 0, rows, :], wq[b, 1, rows, :], wq[b, 2, rows, :]], axis=1)

    def first_norm(s, u):
        def body(r):
            rows = ds(u * HALF + r * 64, 64)
            normed, _ = norm(xs_buf[s, rows, :].astype(F32))
            a1[s, rows, :] = (normed * prm[s, 2:3, :] + prm[s, 4:5, :]).astype(BF16)

        loop(2, body)

    def first_own(s, u):
        normed, inv = norm(xs_buf[s, own(u), :].astype(F32))
        n1[s, u] = normed
        i1[s, u] = jnp.broadcast_to(inv, (R, 128))

    def attention(s, u):
        keys = (u + 1) * HALF
        rows = stream(u)

        def body(h):
            b = 2 * h + s
            bias = jnp.concatenate(
                [prm[b, 7:8, 0:128], jnp.zeros((1, 128), F32), prm[b, 7:8, 128:256]], axis=1
            )
            qkv[s, h, rows, :] = (dot_nn(a1[s, rows, :], planes(b, slice(None))) + bias).astype(BF16)
            query = qkv[s, h, rows, 0:128]
            key, value = qkv[s, h, 0:keys, 128:256], qkv[s, h, 0:keys, 256:384]
            parts = []
            for e in (0, 1):
                scores = dot_nt(pick_head(query, e), key) * SCALE + mask[rows, 0:keys]
                weights = jnp.exp(scores - jnp.max(scores, axis=-1, keepdims=True))
                probs = (weights / jnp.sum(weights, axis=-1, keepdims=True)).astype(BF16)
                prob[s, h, e, rows, 0:keys] = probs
                parts.append(dot_nn(probs, value))
            mix[s, h, rows, :] = jnp.where(low_lanes(HALF), parts[0], parts[1]).astype(BF16)

        loop(2, body)

    def partial(k, u, tile):
        rows = stream(u)

        def body(n):
            cols = ds(n * 256, 256)
            value = tile(rows, cols)
            acc[rows, cols] = value
            rs_out[k // 2, rows, cols] = value.astype(BF16)

        loop(4, body)
        rs_start(k, u)

    def feed_up(s, u):
        rows = stream(u)

        def body(i):
            h, n = lax.div(i, 2), lax.rem(i, 2)
            b = 2 * h + s
            cols = ds(n * 256, 256)
            v = dot_nn(a2[s, rows, :], wu[b, :, cols]) + prm[b, 6:7, cols]
            th = jnp.tanh(GELU_COEF * (v + CUBIC_COEF * v * v * v))
            hid[s, h, rows, cols] = (0.5 * v * (1.0 + th)).astype(BF16)
            slope[s, h, rows, cols] = 0.5 * (1.0 + th) + 0.5 * v * (1.0 - th * th) * GELU_COEF * (
                1.0 + 3.0 * CUBIC_COEF * v * v
            )

        loop(4, body)

    def forward(s, hooks):
        k = 4 * s
        target = xs_buf.at[1] if s == 0 else xo
        for u in (0, 1):
            if s == 1:
                ag_finish(3, u, xs_buf.at[1])
            first_norm(s, u)
            if u == 0:
                hooks[0]()
                w_ready(s, WQ)
            attention(s, u)
            if u == 0:
                hooks[1]()
                w_ready(s, WO)
            partial(
                k, u,
                lambda rows, cols: dot_nn(mix[s, 0, rows, :], wo[s, :, cols])
                + dot_nn(mix[s, 1, rows, :], wo[s + 2, :, cols]),
            )
        hooks[2]()
        for u in (0, 1):
            first_own(s, u)
            middle = xs_buf[s, own(u), :].astype(F32) + rs_finish(k, u) + prm[s, 0:1, :]
            yrow[u] = middle
            normed, inv = norm(middle)
            a2[s, own(u), :] = (normed * prm[s, 3:4, :] + prm[s, 5:6, :]).astype(BF16)
            ag_start(k + 1, u, a2.at[s])
            n2[s, u] = normed
            i2[s, u] = jnp.broadcast_to(inv, (R, 128))
        hooks[3]()
        w_ready(s, WU)
        for u in (0, 1):
            ag_finish(k + 1, u, a2.at[s])
            feed_up(s, u)
            if u == 0:
                hooks[4]()
                w_ready(s, WD)
            partial(
                k + 2, u,
                lambda rows, cols: dot_nn(hid[s, 0, rows, :], wd[s, :, cols])
                + dot_nn(hid[s, 1, rows, :], wd[s + 2, :, cols]),
            )
        hooks[5]()
        for u in (0, 1):
            target[own(u), :] = (yrow[u] + rs_finish(k + 2, u) + prm[s, 1:2, :]).astype(BF16)
            ag_start(k + 3, u, target)

    load_x.wait()
    for d in (1, 2, 3):
        send_prm(d).wait_recv()

    def f0_0():
        w_spread(0, WQ)
        w_spread(0, WO)
        w_hand_over(0, WQ)

    def f0_1():
        w_hand_over(0, WO)

    def f0_2():
        w_send_all(1)
        w_spread(0, WU)

    def f0_3():
        w_hand_over(0, WU)
        w_spread(0, WD)

    def f0_4():
        w_hand_over(0, WD)

    def f0_5():
        w_spread(1, WQ)
        w_spread(1, WO)

    def f1_0():
        w_hand_over(1, WQ)
        w_hand_over(1, WO)

    def f1_2():
        out_start(0, 0, xs_buf.at[1], so_out)
        w_spread(1, WU)

    def f1_3():
        w_hand_over(1, WU)
        w_spread(1, WD)

    def f1_4():
        w_hand_over(1, WD)

    def nothing():
        pass

    forward(0, [f0_0, f0_1, f0_2, f0_3, f0_4, f0_5])
    forward(1, [f1_0, nothing, f1_2, f1_3, f1_4, nothing])
    load_g.wait()

    def attention_back(s, u):
        rows = stream(u)
        keys = (u + 1) * HALF

        def body(h):
            grad_mix = dot_nt(dyb[s, rows, :], wo[2 * h + s]).astype(BF16)
            query = qkv[s, h, rows, 0:128]
            key, value = qkv[s, h, 0:keys, 128:256], qkv[s, h, 0:keys, 256:384]
            parts = []
            for e in (0, 1):
                probs = prob[s, h, e, rows, 0:keys]
                wide = probs.astype(F32)
                grad_prob = dot_nt(pick_head(grad_mix, e), value)
                delta = jnp.sum(wide * grad_prob, axis=-1, keepdims=True)
                grad_scores = (wide * (grad_prob - delta) * SCALE).astype(BF16)
                parts.append((dot_nn(grad_scores, key), dot_tn(grad_scores, query), dot_tn(probs, grad_mix)))
            dqkv[h, rows, 0:128] = jnp.where(low_lanes(HALF), parts[0][0], parts[1][0]).astype(BF16)
            for j in (1, 2):
                both = jnp.where(low_lanes(keys), parts[0][j], parts[1][j])
                cols = slice(j * 128, j * 128 + 128)
                if u == 1:
                    dqkv[h, rows, cols] = both[HALF:, :].astype(BF16)
                    dkv[h, :, (j - 1) * 128 : j * 128] = both[:HALF, :]
                else:
                    dqkv[h, rows, cols] = (both + dkv[h, :, (j - 1) * 128 : j * 128]).astype(BF16)

        loop(2, body)

    def add_row(s, i, value):
        sm[s, i : i + 1, :] = sm[s, i : i + 1, :] + jnp.sum(value, axis=0, keepdims=True)

    def backward(s, k, hooks):
        for u in (1, 0):
            rows = stream(u)
            if s == 0:
                ag_finish(11, u, g_buf.at[0])

            def grad_up_tile(i):
                h, n = lax.div(i, 2), lax.rem(i, 2)
                cols = ds(n * 256, 256)
                value = dot_nt(g_buf[s, rows, :], wd[2 * h + s, cols, :]) * slope[s, h, rows, cols]
                du[h, rows, cols] = value.astype(BF16)

            loop(4, grad_up_tile)
            partial(
                k, u,
                lambda rows, cols: dot_nt(du[0, rows, :], wu[s, cols, :]) + dot_nt(du[1, rows, :], wu[s + 2, cols, :]),
            )

        def grad_down(i):
            h, n = lax.div(i, 2), lax.rem(i, 2)
            rows = ds(n * 256, 256)
            gd[s, h, rows, :] = dot_tn(hid[s, h, :, rows], g_buf[s]).astype(BF16)

        loop(4, grad_down)
        gc_start(s, WD)
        hooks[0]()
        for u in (1, 0):
            top = g_buf[s, own(u), :].astype(F32)
            g_second = rs_finish(k, u)
            normed = n2[s, u]
            dy = top + norm_back(g_second, normed, i2[s, u, :, 0:1], prm[s, 3:4, :])
            dyb[s, own(u), :] = dy.astype(BF16)
            ag_start(k + 1, u, dyb.at[s])
            dyrow[u] = dy
            add_row(s, 1, top)
            add_row(s, 3, g_second * normed)
            add_row(s, 5, g_second)
            add_row(s, 0, dy)

        def grad_up(i):
            h, n = lax.div(i, 4), lax.rem(i, 4)
            rows = ds(n * 256, 256)
            gu[s, h, rows, :] = dot_tn(a2[s, :, rows], du[h]).astype(BF16)

        loop(8, grad_up)
        gc_start(s, WU)
        for h in (0, 1):
            sm[s, 6:7, h * 512 : h * 512 + 512] = jnp.sum(du[h].astype(F32), axis=0, keepdims=True)
        hooks[1]()
        for u in (1, 0):
            ag_finish(k + 1, u, dyb.at[s])
            attention_back(s, u)
            partial(
                k + 2, u,
                lambda rows, cols: dot_nt(dqkv[0, rows, :], planes(s, cols)) + dot_nt(dqkv[1, rows, :], planes(s + 2, cols)),
            )

        def grad_qkv(i):
            h, n = lax.div(i, 4), lax.rem(i, 4)
            rows = ds(n * 256, 256)
            value = dot_tn(a1[s, :, rows], dqkv[h]).astype(BF16)
            for j in range(3):
                gq[s, h, j, rows, :] = value[:, j * 128 : j * 128 + 128]

        loop(8, grad_qkv)
        gc_start(s, WQ)
        for h in (0, 1):
            go[s, h] = dot_tn(mix[s, h], dyb[s]).astype(BF16)
        gc_start(s, WO)
        for h in (0, 1):
            sums = jnp.sum(dqkv[h].astype(F32), axis=0, keepdims=True)
            sm[s, 7:8, h * 256 : h * 256 + 128] = sums[:, 0:128]
            sm[s, 7:8, h * 256 + 128 : h * 256 + 256] = sums[:, 256:384]
        hooks[2]()
        target = g_buf.at[0] if s == 1 else ig0
        for u in (1, 0):
            g_first = rs_finish(k + 2, u)
            normed = n1[s, u]
            low = dyrow[u] + norm_back(g_first, normed, i1[s, u, :, 0:1], prm[s, 2:3, :])
            target[own(u), :] = low.astype(BF16)
            if s == 1:
                ag_start(k + 3, u, target)
            else:
                low_start(u)
            add_row(s, 2, g_first * normed)
            add_row(s, 4, g_first)
        hooks[3]()

    def b1_0():
        for u in (0, 1):
            ag_finish(7, u, xo)
        out_start(1, 1, xo, so_out)

    def b1_1():
        stage1(1, WD)

    def b1_2():
        stage1(1, WU)

    def b1_3():
        stage1(1, WQ)
        stage1(1, WO)

    backward(1, 8, [b1_0, b1_1, b1_2, b1_3])

    def b0_0():
        out_start(2, 1, g_buf.at[0], ig_out)
        stage2(1, WU)

    def b0_1():
        stage1(0, WD)
        stage2(1, WD)

    def b0_2():
        stage1(0, WU)
        stage1(0, WQ)
        stage1(0, WO)
        stage3(1, WU)
        stage2(1, WQ)
        stage2(1, WO)

    def b0_3():
        pass

    backward(0, 12, [b0_0, b0_1, b0_2, b0_3])

    def small_copy(i, src, dst, device):
        return remote(src, dst, sm_s.at[i], sm_r.at[i], device)

    small_c = [small_copy(0, sm, smc, core_peer)]
    small_z = [small_copy(d, sm1, smz.at[d - 1], dev(x, y, zp(d), c)) for d in (1, 2, 3)]
    small_y = [small_copy(3 + d, sm2, smy.at[d - 1], dev(x, yp(d), z, c)) for d in (1, 2, 3)]
    small_x = [small_copy(6 + d, sm3, smx.at[d - 1], dev(xp(d), y, z, c)) for d in (1, 2, 3)]

    def start_all(copies):
        for copy in copies:
            copy.start()

    def arrived(copies):
        for copy in copies:
            copy.wait_recv()

    start_all(small_c)
    stage3(1, WD)
    stage3(1, WQ)
    arrived(small_c)
    sm1[...] = sm[...] + smc[...]
    start_all(small_z)
    stage3(1, WO)
    stage2(0, WU)
    stage2(0, WQ)
    arrived(small_z)
    sm2[...] = sm1[...] + smz[0] + smz[1] + smz[2]
    start_all(small_y)
    stage2(0, WD)
    stage2(0, WO)
    for k in range(4):
        stage4(1, k)
    arrived(small_y)
    sm3[...] = sm2[...] + smy[0] + smy[1] + smy[2]
    start_all(small_x)
    stage3(0, WU)
    stage3(0, WQ)
    arrived(small_x)
    mine = sm3[p]
    shared = mine + smx[0, p] + smx[1, p] + smx[2, p]
    row = lax.broadcasted_iota(jnp.int32, (8, D), 0)
    small_out[...] = jnp.where(row < 6, shared, mine)
    stage3(0, WD)
    stage3(0, WO)
    for k in (WU, WQ, WD, WO):
        stage4(0, k)
    for k in (WU, WQ, WD, WO):
        gf_finish(k)

    out_finish(0, 0, xs_buf.at[1], so_out)
    out_finish(1, 1, xo, so_out)
    out_finish(2, 1, g_buf.at[0], ig_out)
    for u in (1, 0):
        low_finish(u)
    for d in (1, 2, 3):
        send_prm(d).wait_send()
        for k in range(4):
            w_send(k, d).wait_send()
    for s in (0, 1):
        for k in range(4):
            if k not in Z_FIRST:
                @pl.when(p == s)
                def _():
                    for d in (1, 2, 3):
                        gz_copy(s, k, 0, d).wait_send()

            def sent(d):
                for j in (0, 1):
                    w_side(k, d, j).wait_send()
                for j in (0, 1, 2):
                    w_pass(k, d, j).wait_send()

            w_each(s, sent)

            for h in (0, 1):
                gc_copy(s, k, h).wait_send()
                if k in Z_FIRST:
                    for d in (1, 2, 3):
                        gz_copy(s, k, h, d).wait_send()

                @pl.when(y != 2 * h + s)
                def _():
                    gy_copy(s, k, h).wait_send()

    gathered = {
        1: a2.at[0], 3: xs_buf.at[1], 5: a2.at[1], 7: xo, 9: dyb.at[1], 11: g_buf.at[0], 13: dyb.at[0],
    }
    for u in (0, 1):
        for d in (1, 2, 3):
            for k in range(0, 16, 2):
                rs_copy(k, u, d).wait_send()
            for k, ref in gathered.items():
                ag_copy(k, u, ref, d).wait_send()
    for copy in small_c + small_z + small_y + small_x:
        copy.wait_send()


def finish_kernel(
    so_in, ig_in, gq_in, go_in, gu_in, gd_in, small_in,
    so_out, ig_out, gq_out, go_out, gu_out, gd_out, outb, downb, gains, shifts, upb, qvb,
    so_buf, ig_buf, gq_buf, go_buf, gu_buf, gd_buf, gq_f, go_f, gu_f, gd_f, l_sem, s_sem,
):
    ins = (gu_in, gd_in, so_in, ig_in, gq_in, go_in)
    bufs = (gu_buf, gd_buf, so_buf, ig_buf, gq_buf, go_buf)
    wide = (gu_f, gd_f, None, None, gq_f, go_f)
    outs = (gu_out, gd_out, so_out, ig_out, gq_out, go_out)
    loads = [pltpu.make_async_copy(ins[i], bufs[i], l_sem.at[i]) for i in range(6)]
    for copy in loads:
        copy.start()
    h = lax.div(lax.axis_index("tensor"), 4)
    outb[...] = small_in[0:1, :]
    downb[...] = small_in[1:2, :]
    gains[...] = small_in[2:4, :]
    shifts[...] = small_in[4:6, :]
    upb[...] = jnp.where(h == 0, small_in[6:7, 0:512], small_in[6:7, 512:1024])
    qvb[0:1, :] = jnp.where(h == 0, small_in[7:8, 0:128], small_in[7:8, 256:384])
    qvb[1:2, :] = jnp.where(h == 0, small_in[7:8, 128:256], small_in[7:8, 384:512])
    stores = []
    for i in range(6):
        loads[i].wait()
        source = bufs[i]
        if wide[i] is not None:
            source = wide[i]
            lead = source.shape[0]
            step = lead if len(source.shape) == 3 else 64

            def body(r):
                if len(source.shape) == 3:
                    rows = ds(r * 128, 128)
                    wide[i][:, rows, :] = bufs[i][:, rows, :].astype(F32)
                else:
                    rows = ds(r * 64, 64)
                    wide[i][rows, :] = bufs[i][rows, :].astype(F32)

            loop(8 if len(source.shape) == 3 else lead // step, body)
        stores.append(pltpu.make_async_copy(source, outs[i], s_sem.at[i]))
        stores[-1].start()
    for copy in stores:
        copy.wait()


def run(x_in, seg, wq, qvb, wo, outb, wu, upb, wd, downb, gain, shift, og):
    any_spec = pl.BlockSpec(memory_space=pl.ANY)
    vmem = pl.BlockSpec(memory_space=pltpu.VMEM)
    V = pltpu.VMEM
    dma = pltpu.SemaphoreType.DMA
    tokens = x_in.shape[0]

    def kinds(lead, shrink):
        return [V(tuple(lead) + shape_of(k, ROWS[k] // shrink), BF16) for k in range(4)]

    scratch = kinds((4,), 1)
    scratch += [
        V((4, 8, D), F32), V((SEQ, SEQ), F32),
        V((2, SEQ, D), BF16), V((2, SEQ, D), BF16), V((2, SEQ, D), BF16), V((2, SEQ, D), BF16), V((2, SEQ, D), BF16),
        V((SEQ, D), BF16), V((SEQ, D), BF16),
        V((2, 2, SEQ, 384), BF16), V((2, 2, 2, SEQ, SEQ), BF16), V((2, 2, SEQ, 128), BF16),
        V((2, 2, SEQ, 512), BF16), V((2, 2, SEQ, 512), F32),
        V((2, SEQ, 512), BF16), V((2, SEQ, 384), BF16), V((2, HALF, 256), F32), V((SEQ, D), F32),
        V((8, SEQ, D), BF16), V((8, 2, 3, R, D), BF16),
        V((2, 2, R, D), F32), V((2, 2, R, D), F32), V((2, 2, R, 128), F32), V((2, 2, R, 128), F32),
        V((2, R, D), F32), V((2, R, D), F32),
    ]
    scratch += kinds((2, 2), 1) + kinds((2, 2), 2)
    scratch += [V((3,) + shape_of(k, ROWS[k] // (8 if k in Z_FIRST else 2)), BF16) for k in range(4)]
    scratch += [V(((2, 2, 3) if k in Z_FIRST else (3,)) + shape_of(k, ROWS[k] // 8), BF16) for k in range(4)]
    scratch += kinds((), 1)
    scratch += [V((2, 8, D), F32)] * 5 + [V((3, 2, 8, D), F32)] * 3
    sems = (96, 96, 12, 12, 24, 24, 36, 36, 3, 3, 6, 16, 16, 16, 12, 60, 60, 12, 12, 4, 4, 4, 10, 10, 9, 9, 3, 30, 30, 2)
    scratch += [dma((n,)) for n in sems]
    grads = [jax.ShapeDtypeStruct(shape_of(k, ROWS[k]), BF16) for k in range(4)]
    rows = jax.ShapeDtypeStruct((tokens, D), BF16)
    parts = pl.pallas_call(
        kernel,
        out_shape=(rows, rows, *grads, jax.ShapeDtypeStruct((8, D), F32)),
        in_specs=[any_spec, vmem, any_spec, vmem, any_spec, vmem, any_spec, vmem, any_spec, vmem, vmem, vmem, any_spec],
        out_specs=(any_spec,) * 6 + (vmem,),
        scratch_shapes=scratch,
        compiler_params=pltpu.CompilerParams(collective_id=0, has_side_effects=True, vmem_limit_bytes=64 * 1024 * 1024),
    )(x_in, seg, wq, qvb, wo, outb, wu, upb, wd, downb, gain, shift, og)

    def f32(*shape):
        return jax.ShapeDtypeStruct(shape, F32)

    return pl.pallas_call(
        finish_kernel,
        out_shape=(
            rows, rows, *[f32(*shape_of(k, ROWS[k])) for k in range(4)],
            f32(1, D), f32(1, D), f32(2, D), f32(2, D), f32(1, 512), f32(2, 128),
        ),
        in_specs=[any_spec] * 6 + [vmem],
        out_specs=(any_spec,) * 6 + (vmem,) * 6,
        scratch_shapes=[
            V((tokens, D), BF16), V((tokens, D), BF16), *kinds((), 1),
            *[V(shape_of(k, ROWS[k]), F32) for k in range(4)], dma((6,)), dma((6,)),
        ],
        compiler_params=pltpu.CompilerParams(vmem_limit_bytes=48 * 1024 * 1024),
    )(*parts)


def on_device(
    section_input, segment_ids, w_qkv, qv_bias, w_out, out_bias, w_up, up_bias, w_down, down_bias, norm_gains,
    norm_shifts, out_grad,
):
    so, ig, gq, go, gu, gd, outb, downb, gains, shifts, upb, qvb = run(
        section_input, segment_ids.reshape(8, 128), w_qkv[0].transpose(1, 0, 2), qv_bias[0], w_out[0], out_bias,
        w_up[0], up_bias, w_down[0], down_bias, norm_gains[0], norm_shifts[0], out_grad,
    )
    return (
        so[None], ig[None], gq.transpose(1, 0, 2)[None], qvb[None], go[None], outb, gu[None], upb, gd[None], downb,
        gains[None], shifts[None],
    )


def solution(mesh):
    placed = (
        P("dp", None),
        P("dp"),
        P("pipe", None, None, "tensor"),
        P("pipe", None, "tensor"),
        P("pipe", "tensor", None),
        P("pipe", None),
        P("pipe", None, "tensor"),
        P("pipe", "tensor"),
        P("pipe", "tensor", None),
        P("pipe", None),
        P("pipe", None, None),
        P("pipe", None, None),
        P("dp", None),
    )
    return jax.shard_map(
        on_device,
        mesh=mesh,
        in_specs=placed,
        out_specs=(
            P("pipe", "dp", None),
            P("pipe", "dp", None),
            P("pipe", None, None, "tensor"),
            P("pipe", None, "tensor"),
            P("pipe", "tensor", None),
            P("pipe", None),
            P("pipe", None, "tensor"),
            P("pipe", "tensor"),
            P("pipe", "tensor", None),
            P("pipe", None),
            P("pipe", None, None),
            P("pipe", None, None),
        ),
        check_vma=False,
    )
```

time: 314 us -> 279 us (0.89)
  Pallas kernels: 293 us -> 270 us
  local copies, waits for them, and re-layouts: 15.3 us -> 6.87 us
  other arithmetic: 4.97 us -> 0 us
    pallas_call x1 -> x2, Pallas kernels: 293 us -> 270 us  [the longest x1 265 us: run(): pl.pallas_call(kernel, out_shape=(rows, rows, *grads, jax.ShapeDtypeStruc...]
    broadcast_in_dim x3 -> x0, other arithmetic: 4.97 us -> none  [the longest x1 1.79 us: on_device(): go.astype(F32)[None]]
    reshape x3 -> x0, local copies, waits for them, and re-layouts: 3.84 us -> none  [the longest x1 1.4 us: on_device(): gq.astype(F32).reshape(1, D, 3, 128)]
    unnamed x18 -> x12, local copies, waits for them, and re-layouts: 8.62 us -> 6.87 us
where the time goes in v3:
time: 279 us; the launch traced here: 278 us
  Pallas kernels  270 us (97%)
  local copies, waits for them, and re-layouts  6.87 us (2%)
    pallas_call x1, Pallas kernels, run(): pl.pallas_call(kernel, out_shape=(rows, rows, *grads, jax.ShapeDtypeStruc...  265 us
    unnamed x12, local copies, waits for them, and re-layouts  6.87 us

profile of v3, /device:TPU:1, one launch (start us, length us, event | category | flops | bytes accessed | tf_op | source)
XLA Modules:
  0.0 278.1 jit_solution(14790325480800909116)
XLA Ops:
  0.6 265.1 %shard_map.220 = (bf16[1024,1024]{1,0:T(8,128)(2,1)}, bf16[1024,1024]{1,0:T(8,128)(2,1)}, bf16[3,1024,128]{2,1,0:T(8,128)(2,1)}, bf16[128,1024]{1,0:T(8,128)(2,1...) custom-call(bf16[1024,1024]{1,0:T(8,128)(2,1)} %x_in.1, s32[8,128]{1,0:T(8,128)} %bitcast.27, ...), custom_call_target="tpu_custom_call" | custom-call | tf_op jit(solution)/shard_map/pallas_call | solution.py:959
  265.7 0.0 copy-start
  265.7 1.6 copy-done
  267.3 0.0 copy-start.1
  267.3 1.2 copy-done.1
  268.6 0.0 copy-start.2
  268.6 1.2 copy-done.2
  269.8 0.0 copy-start.3
  269.8 1.1 copy-done.3
  270.9 0.0 copy-start.4
  270.9 0.9 copy-done.4
  271.9 0.0 copy-start.5
  271.9 0.8 copy-done.5
  272.6 5.3 %shard_map.221 = (bf16[1024,1024]{1,0:T(8,128)(2,1)}, bf16[1024,1024]{1,0:T(8,128)(2,1)}, f32[3,1024,128]{2,1,0:T(8,128)}, f32[128,1024]{1,0:T(8,128)}, f32[1024...) custom-call(bf16[1024,1024]{1,0:T(8,128)(2,1)S(1)} %copy-done, ...), custom_call_target="tpu_custom_call" | custom-call | tf_op jit(solution)/shard_map/pallas_call | solution.py:971
Async XLA Ops:
  265.7 1.6 copy-start
  267.3 1.2 copy-start.1
  268.6 1.2 copy-start.2
  269.8 1.1 copy-start.3
  270.9 0.9 copy-start.4
  271.9 0.8 copy-start.5

commit v4 on v3

--- a/solution.py
+++ b/solution.py
@@ -70,9 +70,9 @@
     so_out, ig_out, gq_out, go_out, gu_out, gd_out, small_out,
     wq, wo, wu, wd, prm, mask, xs_buf, g_buf, a1, a2, dyb, xo, ig0, qkv, prob, mix, hid, slope, du, dqkv, dkv, acc,
     rs_out, rs_in, n1, n2, i1, i2, yrow, dyrow,
-    gq, go, gu, gd, cq, co, cu, cd, yq, yo, yu, yd, zq, zo, zu, zd, fq, fo, fu, fd,
+    gq, go, gu, gd, cq, co, cu, cd, yq, yo, yu, yd, rq, ro, ru, rd, zq, zo, zu, zd, fq, fo, fu, fd,
     sm, sm1, sm2, sm3, smc, smz, smy, smx,
-    x_s, x_r, wy_s, wy_r, wz_s, wz_r, wc_s, wc_r, pr_s, pr_r, loc, gc_s, gc_r, gy_s, gy_r, gz_s, gz_r, ga_s, ga_r,
+    x_s, x_r, wy_s, wy_r, wz_s, wz_r, wc_s, wc_r, wr_s, wr_r, pr_s, pr_r, loc, gc_s, gc_r, gy_s, gy_r, ry_s, ry_r, gz_s, gz_r, ga_s, ga_r,
     gf_s, gf_r, gl, sm_s, sm_r, o_s, o_r, o_l, d_s, d_r, d_l,
 ):
     p = lax.axis_index("pipe")
@@ -113,6 +113,7 @@
     c_all = (cq, co, cu, cd)
     y_all = (yq, yo, yu, yd)
     z_all = (zq, zo, zu, zd)
+    r_all = (rq, ro, ru, rd)
     fin = (fq, fo, fu, fd)
     g_outs = (gq_out, go_out, gu_out, gd_out)
     grid_peers = [(dx, dy) for dx in range(4) for dy in range(4) if (dx, dy) != (0, 0)]
@@ -179,11 +180,21 @@
         block = w_block(k, d, quarter_rows(k, even) if j == 0 else eighth_rows(k, 1 - even, j - 1))
         return remote(block, block, wc_s.at[i], wc_r.at[i], core_peer)
 
+    def w_relay(k, j):
+        block = w_block(k, 1 if j == 0 else 3, eighth_rows(k, even, j))
+        i = k * 2 + j
+        return remote(block, block, wr_s.at[i], wr_r.at[i], dev(x, yp(1 if j == 0 else 3), z, c))
+
+    def w_relayed(k, j):
+        block = w_block(k, 2, eighth_rows(k, even, j))
+        i = k * 2 + j
+        return remote(block, block, wr_s.at[i], wr_r.at[i], dev(x, yp(1 if j == 0 else 3), z, c))
+
     def w_send_all(s):
         @pl.when(p == s)
         def _():
             for k in range(4):
-                for d in (2, 1, 3):
+                for d in (1, 3):
                     w_send(k, d).start()
 
     def w_each(s, act):
@@ -198,9 +209,16 @@
 
     def w_spread(s, k):
         def act(d):
-            w_send(k, d).wait_recv()
-            for j in (0, 1):
-                w_side(k, d, j).start()
+            if d == 2:
+                w_relayed(k, 0).wait_recv()
+                w_side(k, d, 0).start()
+                w_relayed(k, 1).wait_recv()
+                w_side(k, d, 1).start()
+            else:
+                w_send(k, d).wait_recv()
+                w_relay(k, 0 if d == 1 else 1).start()
+                for j in (0, 1):
+                    w_side(k, d, j).start()
             w_pass(k, d, 0).start()
 
         w_each(s, act)
@@ -351,24 +369,50 @@
     def piece(k, zz):
         return at(k, pl.ds(pl.multiple_of(piece_base(k, zz), 16), ROWS[k] // 8))
 
-    def gy_copy(s, k, h):
-        d = lax.rem(2 * h + s - y + 4, 4)
-        i = (s * 4 + k) * 2 + h
-        rows = piece(k, z) if k in Z_FIRST else at(k, half_rows(k, c))
+    def region(k):
+        return (piece_base(k, z), ROWS[k] // 8) if k in Z_FIRST else (c * (ROWS[k] // 2), ROWS[k] // 2)
+
+    def y_side(j):
+        return yp(1 if j == 0 else 3)
+
+    def relay_copy(s, k, j):
+        base, n = region(k)
+        rows = at(k, pl.ds(pl.multiple_of(base + j * (n // 2), 16), n // 2))
+        i = k * 2 + j
         return remote(
-            g_all[k].at[(s, h) + rows], y_all[k].at[d - 1], gy_s.at[i], gy_r.at[k * 3 + d - 1],
-            dev(x, 2 * h + s, z, c),
+            g_all[k].at[(s, 1 - h_me) + rows], r_all[k].at[j], ry_s.at[i], ry_r.at[i], dev(x, y_side(j), z, c)
         )
 
-    def gy_arrived(k):
-        for d in (1, 3, 2):
-            slot = y_all[k].at[d - 1]
-            remote(slot, slot, gy_s.at[0], gy_r.at[k * 3 + d - 1], dev(x, yp(d), z, c)).wait_recv()
-
-    def gy_start(s, k, h):
-        @pl.when(y != 2 * h + s)
-        def _():
-            gy_copy(s, k, h).start()
+    def main_copy(s, k, j):
+        base, n = region(k)
+        rows = at(k, pl.ds(pl.multiple_of(base, 16), n))
+        i = k * 2 + j
+        block = lax.div(y_side(j), 2)
+        return remote(
+            g_all[k].at[(s, block) + rows], y_all[k].at[j], gy_s.at[i], gy_r.at[i], dev(x, y_side(j), z, c)
+        )
+
+    def relay_start(s, k):
+        @pl.when(p == s)
+        def _():
+            for j in (0, 1):
+                relay_copy(s, k, j).start()
+
+    def main_start(s, k):
+        @pl.when(p != s)
+        def _():
+            base, n = region(k)
+            for j in (0, 1):
+                relay_copy(s, k, j).wait_recv()
+                sum_rows(
+                    k, g_all[k].at[s, lax.div(y_side(j), 2)], base + j * (n // 2), [r_all[k].at[j]], n // 2
+                )
+                main_copy(s, k, j).start()
+
+    def main_arrived(s, k):
+        for j in (0, 1):
+            main_copy(s, k, j).wait_recv()
+        return [y_all[k].at[j] for j in (0, 1)]
 
     def gz_copy(s, k, h, d):
         zz = zp(d)
@@ -397,33 +441,36 @@
             if k in Z_FIRST:
                 for d in (2, 1, 3):
                     gz_copy(s, k, h, d).start()
-            else:
-                gy_start(s, k, h)
+        if k not in Z_FIRST:
+            relay_start(s, k)
 
     def stage2(s, k):
-        q = ROWS[k] // 8
         if k in Z_FIRST:
             for h in (0, 1):
                 for d in (1, 3, 2):
                     gz_copy(s, k, h, d).wait_recv()
-                sum_rows(k, g_all[k].at[s, h], piece_base(k, z), [z_all[k].at[s, h, j] for j in range(3)], q)
-                gy_start(s, k, h)
+                slots = [z_all[k].at[s, h, j] for j in range(3)]
+                sum_rows(k, g_all[k].at[s, h], piece_base(k, z), slots, ROWS[k] // 8)
+            relay_start(s, k)
+        else:
+            main_start(s, k)
+
+    def stage3(s, k):
+        if k in Z_FIRST:
+            main_start(s, k)
         else:
             @pl.when(p == s)
             def _():
-                gy_arrived(k)
-                sum_rows(
-                    k, g_all[k].at[s, h_me], c * (4 * q), [y_all[k].at[j] for j in range(3)], 4 * q
-                )
+                slots = main_arrived(s, k)
+                sum_rows(k, g_all[k].at[s, h_me], c * (ROWS[k] // 2), slots, ROWS[k] // 2)
                 for d in (2, 1, 3):
                     gz_copy(s, k, 0, d).start()
 
-    def stage3(s, k):
+    def stage4(s, k):
         @pl.when(p == s)
         def _():
             if k in Z_FIRST:
-                gy_arrived(k)
-                slots = [y_all[k].at[j] for j in range(3)]
+                slots = main_arrived(s, k)
             else:
                 for d in (1, 3, 2):
                     gz_copy(s, k, 0, d).wait_recv()
@@ -432,7 +479,7 @@
             for d in (2, 1, 3):
                 ga_copy(k, d).start()
 
-    def stage4(s, k):
+    def stage5(s, k):
         @pl.when(p == s)
         def _():
             for d in (1, 3, 2):
@@ -756,6 +803,7 @@
 
     def b1_2():
         stage1(1, WU)
+        stage2(1, WD)
 
     def b1_3():
         stage1(1, WQ)
@@ -766,21 +814,27 @@
     def b0_0():
         out_start(2, 1, g_buf.at[0], ig_out)
         stage2(1, WU)
+        stage3(1, WD)
+        stage2(1, WO)
 
     def b0_1():
         stage1(0, WD)
-        stage2(1, WD)
+        stage3(1, WU)
+        stage2(1, WQ)
 
     def b0_2():
         stage1(0, WU)
+        stage2(0, WD)
         stage1(0, WQ)
         stage1(0, WO)
-        stage3(1, WU)
-        stage2(1, WQ)
-        stage2(1, WO)
+        stage3(1, WO)
+        stage3(1, WQ)
+        stage4(1, WD)
 
     def b0_3():
-        pass
+        stage2(0, WU)
+        stage4(1, WU)
+        stage2(0, WO)
 
     backward(0, 12, [b0_0, b0_1, b0_2, b0_3])
 
@@ -801,36 +855,36 @@
             copy.wait_recv()
 
     start_all(small_c)
-    stage3(1, WD)
-    stage3(1, WQ)
+    stage2(0, WQ)
+    stage3(0, WU)
     arrived(small_c)
     sm1[...] = sm[...] + smc[...]
     start_all(small_z)
-    stage3(1, WO)
-    stage2(0, WU)
-    stage2(0, WQ)
+    stage4(1, WO)
+    stage4(1, WQ)
+    stage3(0, WD)
+    stage3(0, WQ)
+    stage3(0, WO)
     arrived(small_z)
     sm2[...] = sm1[...] + smz[0] + smz[1] + smz[2]
     start_all(small_y)
-    stage2(0, WD)
-    stage2(0, WO)
     for k in range(4):
-        stage4(1, k)
+        stage5(1, k)
+    stage4(0, WU)
     arrived(small_y)
     sm3[...] = sm2[...] + smy[0] + smy[1] + smy[2]
     start_all(small_x)
-    stage3(0, WU)
-    stage3(0, WQ)
+    stage4(0, WD)
+    stage4(0, WO)
+    stage4(0, WQ)
     arrived(small_x)
     mine = sm3[p]
     shared = mine + smx[0, p] + smx[1, p] + smx[2, p]
     row = lax.broadcasted_iota(jnp.int32, (8, D), 0)
     small_out[...] = jnp.where(row < 6, shared, mine)
-    stage3(0, WD)
-    stage3(0, WO)
-    for k in (WU, WQ, WD, WO):
-        stage4(0, k)
-    for k in (WU, WQ, WD, WO):
+    for k in (WU, WD, WO, WQ):
+        stage5(0, k)
+    for k in (WU, WD, WO, WQ):
         gf_finish(k)
 
     out_finish(0, 0, xs_buf.at[1], so_out)
@@ -840,8 +894,6 @@
         low_finish(u)
     for d in (1, 2, 3):
         send_prm(d).wait_send()
-        for k in range(4):
-            w_send(k, d).wait_send()
     for s in (0, 1):
         for k in range(4):
             if k not in Z_FIRST:
@@ -851,6 +903,11 @@
                         gz_copy(s, k, 0, d).wait_send()
 
             def sent(d):
+                if d == 2:
+                    for e in (1, 3):
+                        w_send(k, e).wait_send()
+                else:
+                    w_relay(k, 0 if d == 1 else 1).wait_send()
                 for j in (0, 1):
                     w_side(k, d, j).wait_send()
                 for j in (0, 1, 2):
@@ -864,9 +921,14 @@
                     for d in (1, 2, 3):
                         gz_copy(s, k, h, d).wait_send()
 
-                @pl.when(y != 2 * h + s)
+            for j in (0, 1):
+                @pl.when(p == s)
                 def _():
-                    gy_copy(s, k, h).wait_send()
+                    relay_copy(s, k, j).wait_send()
+
+                @pl.when(p != s)
+                def _():
+                    main_copy(s, k, j).wait_send()
 
     gathered = {
         1: a2.at[0], 3: xs_buf.at[1], 5: a2.at[1], 7: xo, 9: dyb.at[1], 11: g_buf.at[0], 13: dyb.at[0],
@@ -948,11 +1010,12 @@
         V((2, R, D), F32), V((2, R, D), F32),
     ]
     scratch += kinds((2, 2), 1) + kinds((2, 2), 2)
-    scratch += [V((3,) + shape_of(k, ROWS[k] // (8 if k in Z_FIRST else 2)), BF16) for k in range(4)]
+    scratch += [V((2,) + shape_of(k, ROWS[k] // (8 if k in Z_FIRST else 2)), BF16) for k in range(4)]
+    scratch += [V((2,) + shape_of(k, ROWS[k] // (16 if k in Z_FIRST else 4)), BF16) for k in range(4)]
     scratch += [V(((2, 2, 3) if k in Z_FIRST else (3,)) + shape_of(k, ROWS[k] // 8), BF16) for k in range(4)]
     scratch += kinds((), 1)
     scratch += [V((2, 8, D), F32)] * 5 + [V((3, 2, 8, D), F32)] * 3
-    sems = (96, 96, 12, 12, 24, 24, 36, 36, 3, 3, 6, 16, 16, 16, 12, 60, 60, 12, 12, 4, 4, 4, 10, 10, 9, 9, 3, 30, 30, 2)
+    sems = (96, 96, 12, 12, 24, 24, 36, 36, 8, 8, 3, 3, 6, 16, 16, 8, 8, 8, 8, 60, 60, 12, 12, 4, 4, 4, 10, 10, 9, 9, 3, 30, 30, 2)
     scratch += [dma((n,)) for n in sems]
     grads = [jax.ShapeDtypeStruct(shape_of(k, ROWS[k]), BF16) for k in range(4)]
     rows = jax.ShapeDtypeStruct((tokens, D), BF16)
@@ -980,7 +1043,7 @@
             V((tokens, D), BF16), V((tokens, D), BF16), *kinds((), 1),
             *[V(shape_of(k, ROWS[k]), F32) for k in range(4)], dma((6,)), dma((6,)),
         ],
-        compiler_params=pltpu.CompilerParams(vmem_limit_bytes=48 * 1024 * 1024),
+        compiler_params=pltpu.CompilerParams(vmem_limit_bytes=62 * 1024 * 1024),
     )(*parts)
 
 

time: 279 us -> 274 us (0.982)
  local copies, waits for them, and re-layouts: 6.87 us -> 0 us
  Pallas kernels: 270 us -> 273 us
    unnamed x12 -> x0, local copies, waits for them, and re-layouts: 6.87 us -> none
where the time goes in v4:
time: 274 us; the launch traced here: 273 us
  Pallas kernels  273 us (100%)
    pallas_call x1, Pallas kernels, run(): pl.pallas_call(kernel, out_shape=(rows, rows, *grads, jax.ShapeDtypeStruc...  265 us
    pallas_call x1, Pallas kernels, run(): pl.pallas_call(finish_kernel, out_shape=(rows, rows, *[f32(*shape_of(k, R...  7.53 us

profile of v4, /device:TPU:1, one launch (start us, length us, event | category | flops | bytes accessed | tf_op | source)
XLA Modules:
  0.0 273.4 jit_solution(5980821211678746136)
XLA Ops:
  0.6 265.0 %shard_map.220 = (bf16[1024,1024]{1,0:T(8,128)(2,1)}, bf16[1024,1024]{1,0:T(8,128)(2,1)}, bf16[3,1024,128]{2,1,0:T(8,128)(2,1)}, bf16[128,1024]{1,0:T(8,128)(2,1...) custom-call(bf16[1024,1024]{1,0:T(8,128)(2,1)} %x_in.1, s32[8,128]{1,0:T(8,128)} %bitcast.27, ...), custom_call_target="tpu_custom_call" | custom-call | tf_op jit(solution)/shard_map/pallas_call | solution.py:1022
  265.7 7.5 %shard_map.221 = (bf16[1024,1024]{1,0:T(8,128)(2,1)}, bf16[1024,1024]{1,0:T(8,128)(2,1)}, f32[3,1024,128]{2,1,0:T(8,128)}, f32[128,1024]{1,0:T(8,128)}, f32[1024...) custom-call(bf16[1024,1024]{1,0:T(8,128)(2,1)} %get-tuple-element.31, ...), custom_call_target="tpu_custom_call" | custom-call | tf_op jit(solution)/shard_map/pallas_call | solution.py:1034

commit v5 on v4

--- a/solution.py
+++ b/solution.py
@@ -190,12 +190,11 @@
         i = k * 2 + j
         return remote(block, block, wr_s.at[i], wr_r.at[i], dev(x, yp(1 if j == 0 else 3), z, c))
 
-    def w_send_all(s):
+    def w_send_kind(s, k):
         @pl.when(p == s)
         def _():
-            for k in range(4):
-                for d in (1, 3):
-                    w_send(k, d).start()
+            for d in (1, 3):
+                w_send(k, d).start()
 
     def w_each(s, act):
         @pl.when(p == s)
@@ -356,6 +355,9 @@
         def body(r):
             here = at(k, pl.ds(pl.multiple_of(base + r * step, 16), step))
             there = at(k, pl.ds(pl.multiple_of(r * step, 16), step))
+            if len(sources) == 1:
+                result[here] = target[here] + sources[0][there]
+                return
             total = target[here].astype(F32)
             for source in sources:
                 total = total + source[there].astype(F32)
@@ -493,9 +495,10 @@
         for d in (1, 2, 3):
             ga_copy(k, d).wait_send()
 
-    w_send_all(0)
-    for d in (1, 2, 3):
+    for d in (1, 3, 2):
         send_prm(d).start()
+    for k in range(4):
+        w_send_kind(0, k)
 
     seg = jnp.concatenate([seg_in[pl.ds(2 * y, 1), :], seg_in[pl.ds(2 * y + 1, 1), :]], axis=1).astype(F32)
     seg_b = jnp.broadcast_to(seg, (SEQ, SEQ))
@@ -631,19 +634,22 @@
 
     def f0_0():
         w_spread(0, WQ)
+        w_send_kind(1, WQ)
         w_spread(0, WO)
+        w_send_kind(1, WO)
         w_hand_over(0, WQ)
 
     def f0_1():
         w_hand_over(0, WO)
 
     def f0_2():
-        w_send_all(1)
         w_spread(0, WU)
+        w_send_kind(1, WU)
 
     def f0_3():
+        w_spread(0, WD)
+        w_send_kind(1, WD)
         w_hand_over(0, WU)
-        w_spread(0, WD)
 
     def f0_4():
         w_hand_over(0, WD)
@@ -651,6 +657,7 @@
     def f0_5():
         w_spread(1, WQ)
         w_spread(1, WO)
+        w_spread(1, WU)
 
     def f1_0():
         w_hand_over(1, WQ)
@@ -658,11 +665,10 @@
 
     def f1_2():
         out_start(0, 0, xs_buf.at[1], so_out)
-        w_spread(1, WU)
+        w_spread(1, WD)
 
     def f1_3():
         w_hand_over(1, WU)
-        w_spread(1, WD)
 
     def f1_4():
         w_hand_over(1, WD)

time: 274 us -> 243 us (0.89)
  Pallas kernels: 273 us -> 242 us
    pallas_call x1, Pallas kernels: 265 us -> 234 us  [run(): pl.pallas_call(kernel, out_shape=(rows, rows, *grads, jax.ShapeDtypeStruc...]
where the time goes in v5:
time: 243 us; the launch traced here: 242 us
  Pallas kernels  242 us (100%)
    pallas_call x1, Pallas kernels, run(): pl.pallas_call(kernel, out_shape=(rows, rows, *grads, jax.ShapeDtypeStruc...  234 us
    pallas_call x1, Pallas kernels, run(): pl.pallas_call(finish_kernel, out_shape=(rows, rows, *[f32(*shape_of(k, R...  7.53 us

profile of v5, /device:TPU:1, one launch (start us, length us, event | category | flops | bytes accessed | tf_op | source)
XLA Modules:
  0.0 242.4 jit_solution(3252066911994912490)
XLA Ops:
  0.6 234.0 %shard_map.220 = (bf16[1024,1024]{1,0:T(8,128)(2,1)}, bf16[1024,1024]{1,0:T(8,128)(2,1)}, bf16[3,1024,128]{2,1,0:T(8,128)(2,1)}, bf16[128,1024]{1,0:T(8,128)(2,1...) custom-call(bf16[1024,1024]{1,0:T(8,128)(2,1)} %x_in.1, s32[8,128]{1,0:T(8,128)} %bitcast.27, ...), custom_call_target="tpu_custom_call" | custom-call | tf_op jit(solution)/shard_map/pallas_call | solution.py:1028
  234.7 7.5 %shard_map.221 = (bf16[1024,1024]{1,0:T(8,128)(2,1)}, bf16[1024,1024]{1,0:T(8,128)(2,1)}, f32[3,1024,128]{2,1,0:T(8,128)}, f32[128,1024]{1,0:T(8,128)}, f32[1024...) custom-call(bf16[1024,1024]{1,0:T(8,128)(2,1)} %get-tuple-element.31, ...), custom_call_target="tpu_custom_call" | custom-call | tf_op jit(solution)/shard_map/pallas_call | solution.py:1040

commit v6 on v5

--- a/solution.py
+++ b/solution.py
@@ -40,7 +40,22 @@
     lax.fori_loop(0, n, lambda i, c: (body(i), c)[1], 0)
 
 
+def unrolled(n, body):
+    for i in range(n):
+        body(i)
+
+
+def div(a, b):
+    return a // b if isinstance(a, int) else lax.div(a, b)
+
+
+def rem(a, b):
+    return a % b if isinstance(a, int) else lax.rem(a, b)
+
+
 def ds(start, size):
+    if isinstance(start, int):
+        return pl.ds(start, size)
     return pl.ds(pl.multiple_of(start, size), size)
 
 
@@ -523,7 +538,7 @@
             normed, _ = norm(xs_buf[s, rows, :].astype(F32))
             a1[s, rows, :] = (normed * prm[s, 2:3, :] + prm[s, 4:5, :]).astype(BF16)
 
-        loop(2, body)
+        unrolled(2, body)
 
     def first_own(s, u):
         normed, inv = norm(xs_buf[s, own(u), :].astype(F32))
@@ -551,7 +566,7 @@
                 parts.append(dot_nn(probs, value))
             mix[s, h, rows, :] = jnp.where(low_lanes(HALF), parts[0], parts[1]).astype(BF16)
 
-        loop(2, body)
+        unrolled(2, body)
 
     def partial(k, u, tile):
         rows = stream(u)
@@ -562,14 +577,14 @@
             acc[rows, cols] = value
             rs_out[k // 2, rows, cols] = value.astype(BF16)
 
-        loop(4, body)
+        unrolled(4, body)
         rs_start(k, u)
 
     def feed_up(s, u):
         rows = stream(u)
 
         def body(i):
-            h, n = lax.div(i, 2), lax.rem(i, 2)
+            h, n = div(i, 2), rem(i, 2)
             b = 2 * h + s
             cols = ds(n * 256, 256)
             v = dot_nn(a2[s, rows, :], wu[b, :, cols]) + prm[b, 6:7, cols]
@@ -579,7 +594,7 @@
                 1.0 + 3.0 * CUBIC_COEF * v * v
             )
 
-        loop(4, body)
+        unrolled(4, body)
 
     def forward(s, hooks):
         k = 4 * s
@@ -634,9 +649,7 @@
 
     def f0_0():
         w_spread(0, WQ)
-        w_send_kind(1, WQ)
         w_spread(0, WO)
-        w_send_kind(1, WO)
         w_hand_over(0, WQ)
 
     def f0_1():
@@ -644,11 +657,11 @@
 
     def f0_2():
         w_spread(0, WU)
-        w_send_kind(1, WU)
 
     def f0_3():
         w_spread(0, WD)
-        w_send_kind(1, WD)
+        for k in range(4):
+            w_send_kind(1, k)
         w_hand_over(0, WU)
 
     def f0_4():
@@ -664,8 +677,8 @@
         w_hand_over(1, WO)
 
     def f1_2():
+        w_spread(1, WD)
         out_start(0, 0, xs_buf.at[1], so_out)
-        w_spread(1, WD)
 
     def f1_3():
         w_hand_over(1, WU)
@@ -706,7 +719,7 @@
                 else:
                     dqkv[h, rows, cols] = (both + dkv[h, :, (j - 1) * 128 : j * 128]).astype(BF16)
 
-        loop(2, body)
+        unrolled(2, body)
 
     def add_row(s, i, value):
         sm[s, i : i + 1, :] = sm[s, i : i + 1, :] + jnp.sum(value, axis=0, keepdims=True)
@@ -718,23 +731,23 @@
                 ag_finish(11, u, g_buf.at[0])
 
             def grad_up_tile(i):
-                h, n = lax.div(i, 2), lax.rem(i, 2)
+                h, n = div(i, 2), rem(i, 2)
                 cols = ds(n * 256, 256)
                 value = dot_nt(g_buf[s, rows, :], wd[2 * h + s, cols, :]) * slope[s, h, rows, cols]
                 du[h, rows, cols] = value.astype(BF16)
 
-            loop(4, grad_up_tile)
+            unrolled(4, grad_up_tile)
             partial(
                 k, u,
                 lambda rows, cols: dot_nt(du[0, rows, :], wu[s, cols, :]) + dot_nt(du[1, rows, :], wu[s + 2, cols, :]),
             )
 
         def grad_down(i):
-            h, n = lax.div(i, 2), lax.rem(i, 2)
+            h, n = div(i, 2), rem(i, 2)
             rows = ds(n * 256, 256)
             gd[s, h, rows, :] = dot_tn(hid[s, h, :, rows], g_buf[s]).astype(BF16)
 
-        loop(4, grad_down)
+        unrolled(4, grad_down)
         gc_start(s, WD)
         hooks[0]()
         for u in (1, 0):
@@ -751,11 +764,11 @@
             add_row(s, 0, dy)
 
         def grad_up(i):
-            h, n = lax.div(i, 4), lax.rem(i, 4)
+            h, n = div(i, 4), rem(i, 4)
             rows = ds(n * 256, 256)
             gu[s, h, rows, :] = dot_tn(a2[s, :, rows], du[h]).astype(BF16)
 
-        loop(8, grad_up)
+        unrolled(8, grad_up)
         gc_start(s, WU)
         for h in (0, 1):
             sm[s, 6:7, h * 512 : h * 512 + 512] = jnp.sum(du[h].astype(F32), axis=0, keepdims=True)
@@ -769,13 +782,13 @@
             )
 
         def grad_qkv(i):
-            h, n = lax.div(i, 4), lax.rem(i, 4)
+            h, n = div(i, 4), rem(i, 4)
             rows = ds(n * 256, 256)
             value = dot_tn(a1[s, :, rows], dqkv[h]).astype(BF16)
             for j in range(3):
                 gq[s, h, j, rows, :] = value[:, j * 128 : j * 128 + 128]
 
-        loop(8, grad_qkv)
+        unrolled(8, grad_qkv)
         gc_start(s, WQ)
         for h in (0, 1):
             go[s, h] = dot_tn(mix[s, h], dyb[s]).astype(BF16)

time: 243 us -> 223 us (0.918)
  Pallas kernels: 242 us -> 222 us
    pallas_call x1, Pallas kernels: 234 us -> 214 us  [run(): pl.pallas_call(kernel, out_shape=(rows, rows, *grads, jax.ShapeDtypeStruc...]
where the time goes in v6:
time: 223 us
  Pallas kernels  222 us (100%)
    pallas_call x1, Pallas kernels, run(): pl.pallas_call(kernel, out_shape=(rows, rows, *grads, jax.ShapeDtypeStruc...  214 us
    pallas_call x1, Pallas kernels, run(): pl.pallas_call(finish_kernel, out_shape=(rows, rows, *[f32(*shape_of(k, R...  7.53 us

profile of v6, /device:TPU:1, one launch (start us, length us, event | category | flops | bytes accessed | tf_op | source)
XLA Modules:
  0.0 222.8 jit_solution(218311022763752128)
XLA Ops:
  0.6 214.4 %shard_map.220 = (bf16[1024,1024]{1,0:T(8,128)(2,1)}, bf16[1024,1024]{1,0:T(8,128)(2,1)}, bf16[3,1024,128]{2,1,0:T(8,128)(2,1)}, bf16[128,1024]{1,0:T(8,128)(2,1...) custom-call(bf16[1024,1024]{1,0:T(8,128)(2,1)} %x_in.1, s32[8,128]{1,0:T(8,128)} %bitcast.27, ...), custom_call_target="tpu_custom_call" | custom-call | tf_op jit(solution)/shard_map/pallas_call | solution.py:1041
  215.1 7.5 %shard_map.221 = (bf16[1024,1024]{1,0:T(8,128)(2,1)}, bf16[1024,1024]{1,0:T(8,128)(2,1)}, f32[3,1024,128]{2,1,0:T(8,128)}, f32[128,1024]{1,0:T(8,128)}, f32[1024...) custom-call(bf16[1024,1024]{1,0:T(8,128)(2,1)} %get-tuple-element.31, ...), custom_call_target="tpu_custom_call" | custom-call | tf_op jit(solution)/shard_map/pallas_call | solution.py:1053

commit v7 on v6

--- a/solution.py
+++ b/solution.py
@@ -21,7 +21,7 @@
 WQ, WO, WU, WD = range(4)
 ROWS = (1024, 128, 1024, 512)
 COLS = (128, 1024, 512, 1024)
-Z_FIRST = (WQ, WU)
+Z_FIRST = (WQ, WU, WD)
 
 
 def dot_nn(a, b):
@@ -806,7 +806,7 @@
             target[own(u), :] = low.astype(BF16)
             if s == 1:
                 ag_start(k + 3, u, target)
-            else:
+            elif u == 1:
                 low_start(u)
             add_row(s, 2, g_first * normed)
             add_row(s, 4, g_first)
@@ -815,35 +815,35 @@
     def b1_0():
         for u in (0, 1):
             ag_finish(7, u, xo)
+        stage1(1, WD)
         out_start(1, 1, xo, so_out)
 
     def b1_1():
-        stage1(1, WD)
-
-    def b1_2():
         stage1(1, WU)
         stage2(1, WD)
 
-    def b1_3():
+    def b1_2():
         stage1(1, WQ)
         stage1(1, WO)
 
+    def b1_3():
+        stage2(1, WO)
+
     backward(1, 8, [b1_0, b1_1, b1_2, b1_3])
 
     def b0_0():
+        stage1(0, WD)
+        stage2(1, WU)
         out_start(2, 1, g_buf.at[0], ig_out)
-        stage2(1, WU)
         stage3(1, WD)
-        stage2(1, WO)
 
     def b0_1():
-        stage1(0, WD)
+        stage1(0, WU)
+        stage2(0, WD)
         stage3(1, WU)
         stage2(1, WQ)
 
     def b0_2():
-        stage1(0, WU)
-        stage2(0, WD)
         stage1(0, WQ)
         stage1(0, WO)
         stage3(1, WO)
@@ -852,8 +852,8 @@
 
     def b0_3():
         stage2(0, WU)
+        stage2(0, WO)
         stage4(1, WU)
-        stage2(0, WO)
 
     backward(0, 12, [b0_0, b0_1, b0_2, b0_3])
 
@@ -874,15 +874,16 @@
             copy.wait_recv()
 
     start_all(small_c)
+    stage3(0, WU)
     stage2(0, WQ)
-    stage3(0, WU)
     arrived(small_c)
     sm1[...] = sm[...] + smc[...]
     start_all(small_z)
+    stage3(0, WQ)
+    low_start(0)
+    stage3(0, WD)
     stage4(1, WO)
     stage4(1, WQ)
-    stage3(0, WD)
-    stage3(0, WQ)
     stage3(0, WO)
     arrived(small_z)
     sm2[...] = sm1[...] + smz[0] + smz[1] + smz[2]

time: 223 us -> 219 us (0.982)
  Pallas kernels: 222 us -> 218 us
    pallas_call x1, Pallas kernels: 214 us -> 210 us  [run(): pl.pallas_call(kernel, out_shape=(rows, rows, *grads, jax.ShapeDtypeStruc...]
where the time goes in v7:
time: 219 us
  Pallas kernels  218 us (100%)
    pallas_call x1, Pallas kernels, run(): pl.pallas_call(kernel, out_shape=(rows, rows, *grads, jax.ShapeDtypeStruc...  210 us
    pallas_call x1, Pallas kernels, run(): pl.pallas_call(finish_kernel, out_shape=(rows, rows, *[f32(*shape_of(k, R...  7.53 us

profile of v7, /device:TPU:1, one launch (start us, length us, event | category | flops | bytes accessed | tf_op | source)
XLA Modules:
  0.0 218.5 jit_solution(16994191752315900416)
XLA Ops:
  0.6 210.1 %shard_map.220 = (bf16[1024,1024]{1,0:T(8,128)(2,1)}, bf16[1024,1024]{1,0:T(8,128)(2,1)}, bf16[3,1024,128]{2,1,0:T(8,128)(2,1)}, bf16[128,1024]{1,0:T(8,128)(2,1...) custom-call(bf16[1024,1024]{1,0:T(8,128)(2,1)} %x_in.1, s32[8,128]{1,0:T(8,128)} %bitcast.27, ...), custom_call_target="tpu_custom_call" | custom-call | tf_op jit(solution)/shard_map/pallas_call | solution.py:1042
  210.8 7.5 %shard_map.221 = (bf16[1024,1024]{1,0:T(8,128)(2,1)}, bf16[1024,1024]{1,0:T(8,128)(2,1)}, f32[3,1024,128]{2,1,0:T(8,128)}, f32[128,1024]{1,0:T(8,128)}, f32[1024...) custom-call(bf16[1024,1024]{1,0:T(8,128)(2,1)} %get-tuple-element.31, ...), custom_call_target="tpu_custom_call" | custom-call | tf_op jit(solution)/shard_map/pallas_call | solution.py:1054
